TPU v7x, 128 devices: a whole 4x4x4 slice. The times are simulated.
128 devices in a mesh: phase: 16 (over x_lo, y, core), space: 8 (over z, x_hi).
Axes of the slice: x: 4 (x_hi: 2, x_lo: 2; x = x_hi * 2 + x_lo), y: 4, z: 4, core: 2. Of those that a mesh axis runs over, the one named last changes fastest.
Arguments:
- volume: bfloat16 [16, 32, 4, 32, 256], P('phase', 'space'), may hold values from -6 to 6
- gain_first: float32 [256], replicated, may hold values from 0.25 to 1.75
- phase_qkv: bfloat16 [256, 768], replicated, may hold values from -0.375 to 0.375
- phase_out: bfloat16 [256, 256], replicated, may hold values from -0.375 to 0.375
- bin_phase: int32 [16], replicated, may hold values from 0 to 15, each once
- phase_bias: float32 [8, 16], replicated, may hold values from -4 to 304
- gain_second: float32 [256], replicated, may hold values from 0.25 to 1.75
- window_qkv: bfloat16 [256, 768], replicated, may hold values from -0.375 to 0.375
- window_out: bfloat16 [256, 256], replicated, may hold values from -0.375 to 0.375
- window_corner: int32 [8, 3], replicated, may hold values from -3 to 0
- window_bias: float32 [8, 64], replicated, may hold values from -4 to 304
- gain_third: float32 [256], replicated, may hold values from 0.25 to 1.75
- mlp_up: bfloat16 [256, 1024], replicated, may hold values from -0.375 to 0.375
- mlp_down: bfloat16 [1024, 256], replicated, may hold values from -0.1875 to 0.1875
Outputs:
- layer_out: bfloat16 [16, 32, 4, 32, 256], P('phase', 'space')
Inputs may be any that keep to these rules, and one draw needn't show every extreme that they name: `bin_phase`: each phase 0 to 15 is held by exactly one bin. `window_corner`: head h's window covers corner to corner + 3 along each dimension.
All inputs are finite; a program needn't handle non-finite values.
Results may differ from a plain program's by a relative error of at most 0.012.
Values may be sent and summed in bfloat16 or wider, within the bound.
A program may use at most 128 MiB of HBM per device.

v0:
```python
import functools
import math

import jax
import jax.numpy as jnp
from jax import lax
from jax.experimental import pallas as pl
from jax.experimental.pallas import tpu as pltpu
from jax.sharding import PartitionSpec as P

MESH = pl.DeviceIdType.MESH
EPSILON = 1e-06
MASKED = -1e30
F32 = jnp.float32
BF16 = jnp.bfloat16


def normed(values, gain):
    mean_sq = jnp.mean(values * values, axis=-1, keepdims=True)
    return (values * lax.rsqrt(mean_sq + EPSILON) * gain).astype(BF16)


def dot(a, b):
    return jnp.dot(a, b, preferred_element_type=F32)


def dot_t(a, b):
    return lax.dot_general(a, b, (((1,), (1,)), ((), ())), preferred_element_type=F32)


def kernel(
    bins,
    slabs,
    bin_phase,
    phase_bias,
    corner,
    window_bias,
    gain1,
    gain2,
    gain3,
    vol,
    w_qkv1_hbm,
    w_out1_hbm,
    w_qkv2_hbm,
    w_out2_hbm,
    w_up_hbm,
    w_down_hbm,
    out,
    w_qkv1,
    w_out1,
    w_qkv2,
    w_out2,
    w_up,
    w_down,
    got,
    sent,
    ext,
    queries,
    keys,
    values,
    phase_table,
    window_table,
    weight_sem,
    local_sem,
    send_sem,
    recv_sem,
):
    me = lax.axis_index("phase")
    slab = lax.axis_index("space")
    planes, blocks = vol.shape[0], vol.shape[1]
    heads = 8
    scale = 1.0 / math.sqrt(32)
    unscale = math.sqrt(32)
    rate = scale * math.log2(math.e)
    reach = planes - 1
    not_first = slab > 0
    not_last = slab < slabs - 1

    weight_copies = [
        pltpu.make_async_copy(source, target, weight_sem.at[i])
        for i, (source, target) in enumerate(
            [
                (w_qkv1_hbm, w_qkv1),
                (w_out1_hbm, w_out1),
                (w_qkv2_hbm, w_qkv2),
                (w_out2_hbm, w_out2),
                (w_up_hbm, w_up),
                (w_down_hbm, w_down),
            ]
        )
    ]
    for copy in weight_copies:
        copy.start()
    own_in = pltpu.make_async_copy(vol.at[:, me], got.at[:, me], local_sem.at[0])
    own_in.start()

    barrier = pltpu.get_barrier_semaphore()

    @pl.loop(1, bins)
    def _(i):
        pl.semaphore_signal(
            barrier, inc=1, device_id={"phase": lax.rem(me + i, bins)}, device_id_type=MESH
        )

    @pl.when(not_first)
    def _():
        @pl.loop(0, bins)
        def _(i):
            pl.semaphore_signal(
                barrier,
                inc=1,
                device_id={"phase": lax.rem(me + i, bins), "space": slab - 1},
                device_id_type=MESH,
            )

    @pl.when(not_last)
    def _():
        @pl.loop(0, bins)
        def _(i):
            pl.semaphore_signal(
                barrier,
                inc=1,
                device_id={"phase": lax.rem(me + i, bins), "space": slab + 1},
                device_id_type=MESH,
            )

    lane = lax.broadcasted_iota(jnp.int32, (1, 128), 1)

    lane_bin = lax.broadcasted_iota(jnp.int32, (bins, 128), 1) // 8
    row_bin = lax.broadcasted_iota(jnp.int32, (bins, 128), 0)
    there = jnp.zeros((bins, 128), jnp.int32)
    here = jnp.zeros((bins, 128), jnp.int32)
    for c in range(bins):
        there = jnp.where(lane_bin == c, bin_phase[c], there)
        here = jnp.where(row_bin == c, bin_phase[c], here)
    gap = there - here
    gap = jnp.where(gap < 0, gap + bins, gap)
    same = (
        lax.broadcasted_iota(jnp.int32, (bins, 8, 128), 1)
        == lax.broadcasted_iota(jnp.int32, (bins, 8, 128), 2) % 8
    )
    for h in range(heads):
        level = jnp.zeros((bins, 128), F32)
        for k in range(bins):
            level = jnp.where(gap == k, phase_bias[h, k] * unscale, level)
        table = jnp.where(same, jnp.broadcast_to(level[:, None, :], (bins, 8, 128)), MASKED)
        phase_table[h] = table.reshape(128, 128)

    row = lax.broadcasted_iota(jnp.int32, (128, 128), 0)
    column = lax.broadcasted_iota(jnp.int32, (128, 128), 1)
    step_x = column // 32 - row // 32
    step_y = column % 32 - row % 32
    window_table[4 * heads] = jnp.full((128, 128), MASKED, F32)

    @pl.loop(0, heads)
    def _(h):
        b = step_x - corner[h, 1]
        c = step_y - corner[h, 2]
        inside = (b >= 0) & (b < 4) & (c >= 0) & (c < 4)
        code = jnp.where(inside, 4 * b + c, 16)
        for a in range(4):
            table = jnp.full((128, 128), MASKED, F32)
            for j in range(16):
                table = jnp.where(code == j, window_bias[h, 16 * a + j] * unscale, table)
            window_table[4 * h + a] = table

    @pl.when(jnp.logical_not(not_first))
    def _():
        ext[0:reach] = jnp.zeros((reach, blocks, 8, 256), BF16)

    @pl.when(jnp.logical_not(not_last))
    def _():
        ext[reach + planes :] = jnp.zeros((reach, blocks, 8, 256), BF16)

    sides = not_first.astype(jnp.int32) + not_last.astype(jnp.int32)
    pl.semaphore_wait(barrier, bins - 1 + bins * sides)

    @pl.loop(1, bins)
    def _(i):
        peer = lax.rem(me + i, bins)
        pltpu.make_async_remote_copy(
            src_ref=vol.at[:, peer],
            dst_ref=got.at[:, me],
            send_sem=send_sem.at[0],
            recv_sem=recv_sem.at[0],
            device_id={"phase": peer},
            device_id_type=MESH,
        ).start()

    own_in.wait()
    weight_copies[0].wait()
    weight_copies[1].wait()
    others = got.at[:, pl.ds(0, bins - 1)]
    pltpu.make_async_copy(others, others, recv_sem.at[0]).wait()

    ones = jnp.ones((128, 128), BF16)
    head_lanes = [(lane // 32) == i for i in range(4)]
    head_keep = [m.astype(F32).astype(BF16) for m in head_lanes]

    @pl.loop(0, planes)
    def _(g):
        stream = got[g].astype(F32).reshape(128, 256)
        triple = dot(normed(stream, gain1[...]), w_qkv1[...]).astype(BF16)
        tiles = []
        for t in range(2):
            q = triple[:, 128 * t : 128 * t + 128]
            k = triple[:, 256 + 128 * t : 384 + 128 * t]
            v = triple[:, 512 + 128 * t : 640 + 128 * t]
            both = jnp.concatenate([v, ones], axis=1)
            top = jnp.zeros((128, 128), F32)
            low = jnp.ones((128, 128), F32)
            for i in range(4):
                z = dot_t(q * head_keep[i], k) + phase_table[4 * t + i]
                peak = jnp.max(z, axis=1, keepdims=True)
                weight = jnp.exp2((z - peak) * rate).astype(BF16)
                summed = dot(weight, both)
                top = jnp.where(head_lanes[i], summed[:, :128], top)
                low = jnp.where(head_lanes[i], summed[:, 128:], low)
            tiles.append((top / low).astype(BF16))
        mixed = jnp.concatenate(tiles, axis=1)
        residual = stream + dot(mixed, w_out1[...])
        sent[g] = residual.astype(BF16).reshape(blocks, 8, 256)

    own_out = pltpu.make_async_copy(
        sent.at[:, me], ext.at[pl.ds(reach, planes), me], local_sem.at[1]
    )
    own_out.start()

    @pl.loop(1, bins)
    def _(i):
        peer = lax.rem(me + i, bins)
        pltpu.make_async_remote_copy(
            src_ref=sent.at[:, peer],
            dst_ref=ext.at[pl.ds(reach, planes), me],
            send_sem=send_sem.at[1],
            recv_sem=recv_sem.at[1],
            device_id={"phase": peer},
            device_id_type=MESH,
        ).start()

    @pl.when(not_last)
    def _():
        @pl.loop(0, bins)
        def _(i):
            peer = lax.rem(me + i, bins)
            pltpu.make_async_remote_copy(
                src_ref=sent.at[pl.ds(planes - reach, reach), peer],
                dst_ref=ext.at[pl.ds(0, reach), me],
                send_sem=send_sem.at[2],
                recv_sem=recv_sem.at[2],
                device_id={"phase": peer, "space": slab + 1},
                device_id_type=MESH,
            ).start()

    @pl.when(not_first)
    def _():
        @pl.loop(0, bins)
        def _(i):
            peer = lax.rem(me + i, bins)
            pltpu.make_async_remote_copy(
                src_ref=sent.at[pl.ds(0, reach), peer],
                dst_ref=ext.at[pl.ds(reach + planes, reach), me],
                send_sem=send_sem.at[3],
                recv_sem=recv_sem.at[3],
                device_id={"phase": peer, "space": slab - 1},
                device_id_type=MESH,
            ).start()

    weight_copies[2].wait()
    own_out.wait()
    others = ext.at[pl.ds(reach, planes), pl.ds(0, bins - 1)]
    pltpu.make_async_copy(others, others, recv_sem.at[1]).wait()

    @pl.loop(0, planes)
    def _(g):
        stream = ext[reach + g].astype(F32).reshape(128, 256)
        triple = dot(normed(stream, gain2[...]), w_qkv2[...]).astype(BF16)
        queries[g] = triple[:, :256]
        keys[reach + g] = triple[:, 256:512]
        values[reach + g] = triple[:, 512:]

    below = ext.at[pl.ds(0, reach)]
    above = ext.at[pl.ds(reach + planes, reach)]

    @pl.when(not_first)
    def _():
        pltpu.make_async_copy(below, below, recv_sem.at[2]).wait()

    @pl.when(not_last)
    def _():
        pltpu.make_async_copy(above, above, recv_sem.at[3]).wait()

    @pl.loop(0, reach)
    def _(g):
        for plane in (g, reach + planes + g):
            stream = ext[plane].astype(F32).reshape(128, 256)
            pair = dot(normed(stream, gain2[...]), w_qkv2[:, 256:]).astype(BF16)
            keys[plane] = pair[:, :256]
            values[plane] = pair[:, 256:]

    for copy in weight_copies[3:]:
        copy.wait()

    depth = planes * slabs

    @pl.loop(0, planes)
    def _(g):
        tiles = []
        for t in range(2):
            lanes = slice(128 * t, 128 * t + 128)
            q = queries[g, :, lanes]
            top = jnp.zeros((128, 128), F32)
            low = jnp.ones((128, 128), F32)
            for i in range(4):
                h = 4 * t + i
                low_z = g + corner[h, 0]
                first = low_z + reach
                k = keys[pl.ds(first, 4), :, lanes].reshape(512, 128)
                v = values[pl.ds(first, 4), :, lanes].reshape(512, 128)
                parts = []
                for a in range(4):
                    z_key = slab * planes + low_z + a
                    outside = (z_key < 0) | (z_key >= depth)
                    parts.append(window_table[jnp.where(outside, 4 * heads, 4 * h + a)])
                z = dot_t(q * head_keep[i], k) + jnp.concatenate(parts, axis=1)
                peak = jnp.max(z, axis=1, keepdims=True)
                weight = jnp.exp2((z - peak) * rate).astype(BF16)
                both = jnp.concatenate([v, jnp.ones((512, 128), BF16)], axis=1)
                summed = dot(weight, both)
                top = jnp.where(head_lanes[i], summed[:, :128], top)
                low = jnp.where(head_lanes[i], summed[:, 128:], low)
            tiles.append((top / low).astype(BF16))
        mixed = jnp.concatenate(tiles, axis=1)
        residual = ext[reach + g].astype(F32).reshape(128, 256) + dot(mixed, w_out2[...])
        hidden = jax.nn.gelu(dot(normed(residual, gain3[...]), w_up[...]), approximate=True)
        final = residual + dot(hidden.astype(BF16), w_down[...])
        out[g] = final.astype(BF16)

    others = got.at[:, pl.ds(0, bins - 1)]
    pltpu.make_async_copy(others, others, send_sem.at[0]).wait()
    pltpu.make_async_copy(others, others, send_sem.at[1]).wait()

    @pl.when(not_last)
    def _():
        pltpu.make_async_copy(below, below, send_sem.at[2]).wait()

    @pl.when(not_first)
    def _():
        pltpu.make_async_copy(above, above, send_sem.at[3]).wait()


def solution(mesh):
    bins, slabs = mesh.shape["phase"], mesh.shape["space"]

    def local(
        volume,
        gain_first,
        phase_qkv,
        phase_out,
        bin_phase,
        phase_bias,
        gain_second,
        window_qkv,
        window_out,
        window_corner,
        window_bias,
        gain_third,
        mlp_up,
        mlp_down,
    ):
        _, planes, extent_x, extent_y, width = volume.shape
        tokens = extent_x * extent_y
        blocks = tokens // 8
        reach = planes - 1
        deep = planes + 2 * reach
        smem = pl.BlockSpec(memory_space=pltpu.SMEM)
        vmem = pl.BlockSpec(memory_space=pltpu.VMEM)
        hbm = pl.BlockSpec(memory_space=pl.ANY)
        weights = (phase_qkv, phase_out, window_qkv, window_out, mlp_up, mlp_down)
        result = pl.pallas_call(
            functools.partial(kernel, bins, slabs),
            out_shape=jax.ShapeDtypeStruct((planes, tokens, width), BF16),
            in_specs=[smem] * 4 + [vmem] * 3 + [hbm] * 7,
            out_specs=vmem,
            scratch_shapes=[pltpu.VMEM(w.shape, BF16) for w in weights]
            + [
                pltpu.VMEM((planes, blocks, 8, width), BF16),
                pltpu.VMEM((planes, blocks, 8, width), BF16),
                pltpu.VMEM((deep, blocks, 8, width), BF16),
                pltpu.VMEM((planes, tokens, width), BF16),
                pltpu.VMEM((deep, tokens, width), BF16),
                pltpu.VMEM((deep, tokens, width), BF16),
                pltpu.VMEM((8, 128, 128), F32),
                pltpu.VMEM((33, 128, 128), F32),
                pltpu.SemaphoreType.DMA((6,)),
                pltpu.SemaphoreType.DMA((2,)),
                pltpu.SemaphoreType.DMA((4,)),
                pltpu.SemaphoreType.DMA((4,)),
            ],
            compiler_params=pltpu.CompilerParams(collective_id=0, has_side_effects=True),
        )(
            bin_phase,
            phase_bias,
            window_corner,
            window_bias,
            gain_first.reshape(1, width),
            gain_second.reshape(1, width),
            gain_third.reshape(1, width),
            volume.reshape(planes, blocks, 8, width),
            *weights,
        )
        return result.reshape(volume.shape)

    split = P("phase", "space", None, None, None)
    return jax.shard_map(
        local,
        mesh=mesh,
        in_specs=(split,) + (P(),) * 13,
        out_specs=split,
        check_vma=False,
    )
```

profile of v0, /device:TPU:1, one launch (start us, length us, event | category | flops | bytes accessed | tf_op | source)
XLA Modules:
  0.0 43.2 jit_solution(5156716463994330880)
XLA Ops:
  0.0 0.0 copy-start
  0.0 0.7 %copy-done = s32[8,3]{0,1:T(4,128)S(1)} copy-done((s32[8,3]{0,1:T(4,128)S(1)}, s32[8,3]{0,1:T(4,128)}, u32[]{:S(2)}) %copy-start) | copy-done | bytes 120
  0.7 0.7 %copy.15.corner = s32[8,3]{1,0:T(8,128)} copy(s32[8,3]{0,1:T(4,128)S(1)} %copy-done) | data formatting | bytes 192 | tf_op args[9]
  1.4 40.2 %shard_map.136 = bf16[4,128,256]{2,1,0:T(8,128)(2,1)} custom-call(s32[16]{0:T(128)} %bin_phase.1, f32[8,16]{1,0:T(8,128)} %phase_bias.1, s32[8,3]{1,0:T(8,128)} %copy.15.corner, f32[8,64]{1,0:T(8,128)} %window_bias.1, f32[1,256]{1,0:T(1,128)} %bitcast.7, f32[1,256]{1,0:T(1,128)} %bitcast.8, f32[1,256]{1,0:T(1,128)} %bitcast.9, ...), custom_call_target="tpu_custom_call" | custom-call | tf_op jit(solution)/shard_map/pallas_call | solution.py:380
  41.5 1.7 %copy.17 = bf16[1,4,4,32,256]{4,3,2,1,0:T(8,128)(2,1)} copy(bf16[1,4,4,32,256]{4,3,2,1,0:T(8,128)(2,1)} %bitcast.5) | data formatting | bytes 524288
Async XLA Ops:
  0.0 0.7 %copy-start = (s32[8,3]{0,1:T(4,128)S(1)}, s32[8,3]{0,1:T(4,128)}, u32[]{:S(2)}) copy-start(s32[8,3]{0,1:T(4,128)} %param.23) | copy-start | bytes 292
where the time goes:
time: 43.4 us; the launch traced here: 43.2 us
  Pallas kernels  40.2 us (93%)
  local copies, waits for them, and re-layouts  3.02 us (7%)
    pallas_call x1, Pallas kernels, local(): pl.pallas_call(functools.partial(kernel, bins, slabs), out_shape=jax.Shap...  40.2 us
    unnamed x4, local copies, waits for them, and re-layouts  3.02 us

commit v1 on v0

v1 whole, which is shorter than its diff:
```python
import functools
import math

import jax
import jax.numpy as jnp
from jax import lax
from jax.experimental import pallas as pl
from jax.experimental.pallas import tpu as pltpu
from jax.sharding import PartitionSpec as P

MESH = pl.DeviceIdType.MESH
EPSILON = 1e-06
MASKED = -1e30
F32 = jnp.float32
BF16 = jnp.bfloat16


def normed(values, gain):
    mean_sq = jnp.mean(values * values, axis=-1, keepdims=True)
    return (values * lax.rsqrt(mean_sq + EPSILON) * gain).astype(BF16)


def dot(a, b):
    return jnp.dot(a, b, preferred_element_type=F32)


def dot_t(a, b):
    return lax.dot_general(a, b, (((1,), (1,)), ((), ())), preferred_element_type=F32)


def kernel(
    bins,
    slabs,
    bin_phase,
    phase_bias,
    corner,
    window_bias,
    gain1_hbm,
    gain2_hbm,
    gain3_hbm,
    vol,
    w_qkv1_hbm,
    w_out1_hbm,
    w_qkv2_hbm,
    w_out2_hbm,
    w_up_hbm,
    w_down_hbm,
    out,
    gain1,
    gain2,
    gain3,
    w_qkv1,
    w_out1,
    w_qkv2,
    w_out2,
    w_up,
    w_down,
    got,
    sent,
    ext,
    queries,
    keys,
    values,
    phase_table,
    window_table,
    weight_sem,
    local_sem,
    send_sem,
    recv_sem,
):
    me = lax.axis_index("phase")
    slab = lax.axis_index("space")
    planes, blocks = vol.shape[0], vol.shape[1]
    heads = 8
    scale = 1.0 / math.sqrt(32)
    unscale = math.sqrt(32)
    rate = scale * math.log2(math.e)
    reach = planes - 1
    not_first = slab > 0
    not_last = slab < slabs - 1

    barrier = pltpu.get_barrier_semaphore()

    @pl.loop(1, bins)
    def _(i):
        pl.semaphore_signal(
            barrier, inc=1, device_id={"phase": lax.rem(me + i, bins)}, device_id_type=MESH
        )

    @pl.when(not_first)
    def _():
        @pl.loop(0, bins)
        def _(i):
            pl.semaphore_signal(
                barrier,
                inc=1,
                device_id={"phase": lax.rem(me + i, bins), "space": slab - 1},
                device_id_type=MESH,
            )

    @pl.when(not_last)
    def _():
        @pl.loop(0, bins)
        def _(i):
            pl.semaphore_signal(
                barrier,
                inc=1,
                device_id={"phase": lax.rem(me + i, bins), "space": slab + 1},
                device_id_type=MESH,
            )

    weight_copies = [
        pltpu.make_async_copy(source, target, weight_sem.at[i])
        for i, (source, target) in enumerate(
            [
                (gain1_hbm, gain1),
                (w_qkv1_hbm, w_qkv1),
                (w_out1_hbm, w_out1),
                (gain2_hbm, gain2),
                (w_qkv2_hbm, w_qkv2),
                (w_out2_hbm, w_out2),
                (gain3_hbm, gain3),
                (w_up_hbm, w_up),
                (w_down_hbm, w_down),
            ]
        )
    ]
    for copy in weight_copies:
        copy.start()
    own_in = pltpu.make_async_copy(vol.at[:, me], got.at[:, me], local_sem.at[0])
    own_in.start()

    lane = lax.broadcasted_iota(jnp.int32, (1, 128), 1)

    lane_bin = lax.broadcasted_iota(jnp.int32, (bins, 128), 1) // 8
    row_bin = lax.broadcasted_iota(jnp.int32, (bins, 128), 0)
    there = jnp.zeros((bins, 128), jnp.int32)
    here = jnp.zeros((bins, 128), jnp.int32)
    for c in range(bins):
        there = jnp.where(lane_bin == c, bin_phase[c], there)
        here = jnp.where(row_bin == c, bin_phase[c], here)
    gap = there - here
    gap = jnp.where(gap < 0, gap + bins, gap)
    same = (
        lax.broadcasted_iota(jnp.int32, (bins, 8, 128), 1)
        == lax.broadcasted_iota(jnp.int32, (bins, 8, 128), 2) % 8
    )
    for h in range(heads):
        level = jnp.zeros((bins, 128), F32)
        for k in range(bins):
            level = jnp.where(gap == k, phase_bias[h, k] * unscale, level)
        table = jnp.where(same, jnp.broadcast_to(level[:, None, :], (bins, 8, 128)), MASKED)
        phase_table[h] = table.reshape(128, 128)

    @pl.when(jnp.logical_not(not_first))
    def _():
        ext[0:reach] = jnp.zeros((reach, blocks, 8, 256), BF16)

    @pl.when(jnp.logical_not(not_last))
    def _():
        ext[reach + planes :] = jnp.zeros((reach, blocks, 8, 256), BF16)

    sides = not_first.astype(jnp.int32) + not_last.astype(jnp.int32)
    pl.semaphore_wait(barrier, bins - 1 + bins * sides)

    half = planes // 2
    for part in range(2):

        @pl.loop(1, bins)
        def _(i):
            peer = lax.rem(me + i, bins)
            pltpu.make_async_remote_copy(
                src_ref=vol.at[pl.ds(half * part, half), peer],
                dst_ref=got.at[pl.ds(half * part, half), me],
                send_sem=send_sem.at[part],
                recv_sem=recv_sem.at[part],
                device_id={"phase": peer},
                device_id_type=MESH,
            ).start()

    row = lax.broadcasted_iota(jnp.int32, (128, 128), 0)
    column = lax.broadcasted_iota(jnp.int32, (128, 128), 1)
    step_x = column // 32 - row // 32
    step_y = column % 32 - row % 32
    window_table[4 * heads] = jnp.full((128, 128), MASKED, F32)

    @pl.loop(0, heads)
    def _(h):
        b = step_x - corner[1, h]
        c = step_y - corner[2, h]
        inside = (b >= 0) & (b < 4) & (c >= 0) & (c < 4)
        code = jnp.where(inside, 4 * b + c, 16)
        for a in range(4):
            table = jnp.full((128, 128), MASKED, F32)
            for j in range(16):
                table = jnp.where(code == j, window_bias[h, 16 * a + j] * unscale, table)
            window_table[4 * h + a] = table

    head_lanes = [(lane // 32) == i for i in range(4)]
    head_keep = [m.astype(F32).astype(BF16) for m in head_lanes]

    def attend(part):
        rows = 128 * half
        stream = got[half * part : half * part + half].astype(F32).reshape(rows, 256)
        triple = dot(normed(stream, gain1[...]), w_qkv1[...]).astype(BF16)
        mixed = []
        for p in range(half):
            tiles = []
            for t in range(2):
                q = triple[128 * p : 128 * p + 128, 128 * t : 128 * t + 128]
                k = triple[128 * p : 128 * p + 128, 256 + 128 * t : 384 + 128 * t]
                v = triple[128 * p : 128 * p + 128, 512 + 128 * t : 640 + 128 * t]
                both = jnp.concatenate([v, jnp.ones((128, 128), BF16)], axis=1)
                stacked = jnp.concatenate([q * keep for keep in head_keep], axis=0)
                z = dot_t(stacked, k) + phase_table[4 * t : 4 * t + 4].reshape(512, 128)
                peak = jnp.max(z, axis=1, keepdims=True)
                weight = jnp.exp2((z - peak) * rate).astype(BF16)
                summed = dot(weight, both)
                top = summed[:128, :128]
                low = summed[:128, 128:]
                for i in range(1, 4):
                    top = jnp.where(head_lanes[i], summed[128 * i : 128 * i + 128, :128], top)
                    low = jnp.where(head_lanes[i], summed[128 * i : 128 * i + 128, 128:], low)
                tiles.append((top / low).astype(BF16))
            mixed.append(jnp.concatenate(tiles, axis=1))
        residual = stream + dot(jnp.concatenate(mixed, axis=0), w_out1[...])
        sent[half * part : half * part + half] = residual.astype(BF16).reshape(half, blocks, 8, 256)

    def hand_on(part):
        here = half * part
        up = max(here, planes - reach)
        up_count = here + half - up
        down_count = min(here + half, reach) - here
        pltpu.make_async_copy(
            sent.at[pl.ds(here, half), me], ext.at[pl.ds(reach + here, half), me], local_sem.at[1 + part]
        ).start()

        @pl.when(not_last)
        def _():
            @pl.loop(0, bins)
            def _(i):
                peer = lax.rem(me + i, bins)
                pltpu.make_async_remote_copy(
                    src_ref=sent.at[pl.ds(up, up_count), peer],
                    dst_ref=ext.at[pl.ds(up - (planes - reach), up_count), me],
                    send_sem=send_sem.at[4 + part],
                    recv_sem=recv_sem.at[4 + part],
                    device_id={"phase": peer, "space": slab + 1},
                    device_id_type=MESH,
                ).start()

        @pl.when(not_first)
        def _():
            @pl.loop(0, bins)
            def _(i):
                peer = lax.rem(me + i, bins)
                pltpu.make_async_remote_copy(
                    src_ref=sent.at[pl.ds(here, down_count), peer],
                    dst_ref=ext.at[pl.ds(reach + planes + here, down_count), me],
                    send_sem=send_sem.at[6 + part],
                    recv_sem=recv_sem.at[6 + part],
                    device_id={"phase": peer, "space": slab - 1},
                    device_id_type=MESH,
                ).start()

        @pl.loop(1, bins)
        def _(i):
            peer = lax.rem(me + i, bins)
            pltpu.make_async_remote_copy(
                src_ref=sent.at[pl.ds(here, half), peer],
                dst_ref=ext.at[pl.ds(reach + here, half), me],
                send_sem=send_sem.at[2 + part],
                recv_sem=recv_sem.at[2 + part],
                device_id={"phase": peer},
                device_id_type=MESH,
            ).start()

    def arrived(ref, sem):
        pltpu.make_async_copy(ref, ref, sem).wait()

    own_in.wait()
    for copy in weight_copies[:3]:
        copy.wait()
    for part in range(2):
        arrived(got.at[pl.ds(0, half), pl.ds(0, bins - 1)], recv_sem.at[part])
        attend(part)
        hand_on(part)

    for copy in weight_copies[3:5]:
        copy.wait()

    def project(plane, inner):
        stream = ext[plane].astype(F32).reshape(128, 256)
        if inner is None:
            pair = dot(normed(stream, gain2[...]), w_qkv2[:, 256:]).astype(BF16)
            keys[plane] = pair[:, :256]
            values[plane] = pair[:, 256:]
        else:
            triple = dot(normed(stream, gain2[...]), w_qkv2[...]).astype(BF16)
            queries[inner] = triple[:, :256]
            keys[plane] = triple[:, 256:512]
            values[plane] = triple[:, 512:]

    for part in range(2):
        pltpu.make_async_copy(
            sent.at[pl.ds(0, half), me], ext.at[pl.ds(reach, half), me], local_sem.at[1 + part]
        ).wait()
        arrived(got.at[pl.ds(0, half), pl.ds(0, bins - 1)], recv_sem.at[2 + part])

        @pl.loop(half * part, half * part + half)
        def _(g):
            project(reach + g, g)

    for part in range(2):
        here = half * part
        up = max(here, planes - reach)
        up_count = here + half - up
        down_count = min(here + half, reach) - here

        @pl.when(not_first)
        def _():
            arrived(ext.at[pl.ds(0, up_count)], recv_sem.at[4 + part])

        @pl.when(not_last)
        def _():
            arrived(ext.at[pl.ds(0, down_count)], recv_sem.at[6 + part])

        first = up - (planes - reach)

        @pl.loop(first, first + up_count)
        def _(g):
            project(g, None)

        @pl.loop(reach + planes + here, reach + planes + here + down_count)
        def _(g):
            project(g, None)

    for copy in weight_copies[5:]:
        copy.wait()

    depth = planes * slabs

    @pl.loop(0, planes)
    def _(g):
        tiles = []
        for t in range(2):
            lanes = slice(128 * t, 128 * t + 128)
            q = queries[g, :, lanes]
            top = jnp.zeros((128, 128), F32)
            low = jnp.ones((128, 128), F32)
            for i in range(4):
                h = 4 * t + i
                low_z = g + corner[0, h]
                first = low_z + reach
                k = keys[pl.ds(first, 4), :, lanes].reshape(512, 128)
                v = values[pl.ds(first, 4), :, lanes].reshape(512, 128)
                parts = []
                for a in range(4):
                    z_key = slab * planes + low_z + a
                    outside = (z_key < 0) | (z_key >= depth)
                    parts.append(window_table[jnp.where(outside, 4 * heads, 4 * h + a)])
                z = dot_t(q * head_keep[i], k) + jnp.concatenate(parts, axis=1)
                peak = jnp.max(z, axis=1, keepdims=True)
                weight = jnp.exp2((z - peak) * rate).astype(BF16)
                both = jnp.concatenate([v, jnp.ones((512, 128), BF16)], axis=1)
                summed = dot(weight, both)
                top = jnp.where(head_lanes[i], summed[:, :128], top)
                low = jnp.where(head_lanes[i], summed[:, 128:], low)
            tiles.append((top / low).astype(BF16))
        mixed = jnp.concatenate(tiles, axis=1)
        residual = ext[reach + g].astype(F32).reshape(128, 256) + dot(mixed, w_out2[...])
        hidden = jax.nn.gelu(dot(normed(residual, gain3[...]), w_up[...]), approximate=True)
        final = residual + dot(hidden.astype(BF16), w_down[...])
        out[g] = final

    for part in range(2):
        here = half * part
        up_count = here + half - max(here, planes - reach)
        down_count = min(here + half, reach) - here
        arrived(got.at[pl.ds(0, half), pl.ds(0, bins - 1)], send_sem.at[part])
        arrived(got.at[pl.ds(0, half), pl.ds(0, bins - 1)], send_sem.at[2 + part])

        @pl.when(not_last)
        def _():
            arrived(ext.at[pl.ds(0, up_count)], send_sem.at[4 + part])

        @pl.when(not_first)
        def _():
            arrived(ext.at[pl.ds(0, down_count)], send_sem.at[6 + part])


def solution(mesh):
    bins, slabs = mesh.shape["phase"], mesh.shape["space"]

    def local(
        volume,
        gain_first,
        phase_qkv,
        phase_out,
        bin_phase,
        phase_bias,
        gain_second,
        window_qkv,
        window_out,
        window_corner,
        window_bias,
        gain_third,
        mlp_up,
        mlp_down,
    ):
        _, planes, extent_x, extent_y, width = volume.shape
        tokens = extent_x * extent_y
        blocks = tokens // 8
        reach = planes - 1
        deep = planes + 2 * reach
        smem = pl.BlockSpec(memory_space=pltpu.SMEM)
        vmem = pl.BlockSpec(memory_space=pltpu.VMEM)
        hbm = pl.BlockSpec(memory_space=pl.ANY)
        weights = (phase_qkv, phase_out, window_qkv, window_out, mlp_up, mlp_down)
        result = pl.pallas_call(
            functools.partial(kernel, bins, slabs),
            out_shape=jax.ShapeDtypeStruct((planes, tokens, width), F32),
            in_specs=[smem] * 4 + [hbm] * 10,
            out_specs=vmem,
            scratch_shapes=[pltpu.VMEM((1, width), F32)] * 3
            + [pltpu.VMEM(w.shape, BF16) for w in weights]
            + [
                pltpu.VMEM((planes, blocks, 8, width), BF16),
                pltpu.VMEM((planes, blocks, 8, width), BF16),
                pltpu.VMEM((deep, blocks, 8, width), BF16),
                pltpu.VMEM((planes, tokens, width), BF16),
                pltpu.VMEM((deep, tokens, width), BF16),
                pltpu.VMEM((deep, tokens, width), BF16),
                pltpu.VMEM((8, 128, 128), F32),
                pltpu.VMEM((33, 128, 128), F32),
                pltpu.SemaphoreType.DMA((9,)),
                pltpu.SemaphoreType.DMA((3,)),
                pltpu.SemaphoreType.DMA((8,)),
                pltpu.SemaphoreType.DMA((8,)),
            ],
            compiler_params=pltpu.CompilerParams(collective_id=0, has_side_effects=True),
        )(
            bin_phase,
            phase_bias,
            window_corner.T,
            window_bias,
            gain_first.reshape(1, width),
            gain_second.reshape(1, width),
            gain_third.reshape(1, width),
            volume.reshape(planes, blocks, 8, width),
            *weights,
        )
        return result.astype(BF16).reshape(volume.shape)

    split = P("phase", "space", None, None, None)
    return jax.shard_map(
        local,
        mesh=mesh,
        in_specs=(split,) + (P(),) * 13,
        out_specs=split,
        check_vma=False,
    )
```

time: 43.4 us -> 37.4 us (0.86)
  Pallas kernels: 40.2 us -> 35.4 us
  local copies, waits for them, and re-layouts: 3.02 us -> 0 us
  other arithmetic: 0 us -> 1.77 us
    pallas_call x1, Pallas kernels: 40.2 us -> 35.4 us  [local(): pl.pallas_call(functools.partial(kernel, bins, slabs), out_shape=jax.Shap...]
    unnamed x4 -> x0, local copies, waits for them, and re-layouts: 3.02 us -> none
    convert_element_type x0 -> x1, other arithmetic: none -> 1.77 us  [local(): return result.astype(BF16).reshape(volume.shape)]
where the time goes in v1:
time: 37.4 us; the launch traced here: 37.2 us
  Pallas kernels  35.4 us (95%)
  other arithmetic  1.77 us (5%)
    pallas_call x1, Pallas kernels, local(): pl.pallas_call(functools.partial(kernel, bins, slabs), out_shape=jax.Shap...  35.4 us
    convert_element_type x1, other arithmetic, local(): return result.astype(BF16).reshape(volume.shape)  1.77 us

profile of v1, /device:TPU:1, one launch (start us, length us, event | category | flops | bytes accessed | tf_op | source)
XLA Modules:
  0.0 37.2 jit_solution(12097532145749594868)
XLA Ops:
  0.0 35.4 %shard_map.136 = f32[4,128,256]{2,1,0:T(8,128)} custom-call(s32[16]{0:T(128)} %bin_phase.1, f32[8,16]{1,0:T(8,128)} %phase_bias.1, s32[3,8]{1,0:T(4,128)} %bitcast.7, f32[8,64]{1,0:T(8,128)} %window_bias.1, f32[1,256]{1,0:T(1,128)} %bitcast.8, f32[1,256]{1,0:T(1,128)} %bitcast.9, f32[1,256]{1,0:T(1,128)} %bitcast.10, bf16[4,16,8,256]{3,2,1,0:T(8,128)(2,1)} %bitcast.6, ...), custom_call_target="tpu_custom_call" | custom-call | tf_op jit(solution)/shard_map/pallas_call | solution.py:420
  35.5 1.8 %convert_element_type.3 = bf16[4,128,256]{2,1,0:T(8,128)(2,1)} convert(f32[4,128,256]{2,1,0:T(8,128)} %shard_map.136) | non-fusion elementwise | flops 131072 | bytes 786432 | tf_op jit(solution)/shard_map/convert_element_type | solution.py:453

commit v2 on v1

--- a/solution.py
+++ b/solution.py
@@ -89,25 +89,11 @@
 
     @pl.when(not_first)
     def _():
-        @pl.loop(0, bins)
-        def _(i):
-            pl.semaphore_signal(
-                barrier,
-                inc=1,
-                device_id={"phase": lax.rem(me + i, bins), "space": slab - 1},
-                device_id_type=MESH,
-            )
+        pl.semaphore_signal(barrier, inc=1, device_id={"space": slab - 1}, device_id_type=MESH)
 
     @pl.when(not_last)
     def _():
-        @pl.loop(0, bins)
-        def _(i):
-            pl.semaphore_signal(
-                barrier,
-                inc=1,
-                device_id={"phase": lax.rem(me + i, bins), "space": slab + 1},
-                device_id_type=MESH,
-            )
+        pl.semaphore_signal(barrier, inc=1, device_id={"space": slab + 1}, device_id_type=MESH)
 
     weight_copies = [
         pltpu.make_async_copy(source, target, weight_sem.at[i])
@@ -161,7 +147,7 @@
         ext[reach + planes :] = jnp.zeros((reach, blocks, 8, 256), BF16)
 
     sides = not_first.astype(jnp.int32) + not_last.astype(jnp.int32)
-    pl.semaphore_wait(barrier, bins - 1 + bins * sides)
+    pl.semaphore_wait(barrier, bins - 1 + sides)
 
     half = planes // 2
     for part in range(2):

time: 37.4 us -> 35.6 us (0.952)
  Pallas kernels: 35.4 us -> 33.6 us
    pallas_call x1, Pallas kernels: 35.4 us -> 33.6 us  [local(): pl.pallas_call(functools.partial(kernel, bins, slabs), out_shape=jax.Shap...]
where the time goes in v2:
time: 35.6 us; the launch traced here: 35.4 us
  Pallas kernels  33.6 us (94%)
  other arithmetic  1.77 us (5%)
    pallas_call x1, Pallas kernels, local(): pl.pallas_call(functools.partial(kernel, bins, slabs), out_shape=jax.Shap...  33.6 us
    convert_element_type x1, other arithmetic, local(): return result.astype(BF16).reshape(volume.shape)  1.77 us

profile of v2, /device:TPU:1, one launch (start us, length us, event | category | flops | bytes accessed | tf_op | source)
XLA Modules:
  0.0 35.4 jit_solution(2209156148637650325)
XLA Ops:
  0.0 33.6 %shard_map.136 = f32[4,128,256]{2,1,0:T(8,128)} custom-call(s32[16]{0:T(128)} %bin_phase.1, f32[8,16]{1,0:T(8,128)} %phase_bias.1, s32[3,8]{1,0:T(4,128)} %bitcast.7, f32[8,64]{1,0:T(8,128)} %window_bias.1, f32[1,256]{1,0:T(1,128)} %bitcast.8, f32[1,256]{1,0:T(1,128)} %bitcast.9, f32[1,256]{1,0:T(1,128)} %bitcast.10, bf16[4,16,8,256]{3,2,1,0:T(8,128)(2,1)} %bitcast.6, ...), custom_call_target="tpu_custom_call" | custom-call | tf_op jit(solution)/shard_map/pallas_call | solution.py:406
  33.6 1.8 %convert_element_type.3 = bf16[4,128,256]{2,1,0:T(8,128)(2,1)} convert(f32[4,128,256]{2,1,0:T(8,128)} %shard_map.136) | non-fusion elementwise | flops 131072 | bytes 786432 | tf_op jit(solution)/shard_map/convert_element_type | solution.py:439

commit v3 on v2

--- a/solution.py
+++ b/solution.py
@@ -31,10 +31,10 @@
 def kernel(
     bins,
     slabs,
-    bin_phase,
-    phase_bias,
-    corner,
-    window_bias,
+    bin_phase_hbm,
+    phase_bias_hbm,
+    corner_hbm,
+    window_bias_hbm,
     gain1_hbm,
     gain2_hbm,
     gain3_hbm,
@@ -46,6 +46,10 @@
     w_up_hbm,
     w_down_hbm,
     out,
+    bin_phase,
+    phase_bias,
+    corner,
+    window_bias,
     gain1,
     gain2,
     gain3,
@@ -63,6 +67,7 @@
     values,
     phase_table,
     window_table,
+    table_sem,
     weight_sem,
     local_sem,
     send_sem,
@@ -95,6 +100,19 @@
     def _():
         pl.semaphore_signal(barrier, inc=1, device_id={"space": slab + 1}, device_id_type=MESH)
 
+    table_copies = [
+        pltpu.make_async_copy(source, target, table_sem.at[i])
+        for i, (source, target) in enumerate(
+            [
+                (bin_phase_hbm, bin_phase),
+                (phase_bias_hbm, phase_bias),
+                (corner_hbm, corner),
+                (window_bias_hbm, window_bias),
+            ]
+        )
+    ]
+    for copy in table_copies:
+        copy.start()
     weight_copies = [
         pltpu.make_async_copy(source, target, weight_sem.at[i])
         for i, (source, target) in enumerate(
@@ -116,6 +134,8 @@
     own_in = pltpu.make_async_copy(vol.at[:, me], got.at[:, me], local_sem.at[0])
     own_in.start()
 
+    for copy in table_copies:
+        copy.wait()
     lane = lax.broadcasted_iota(jnp.int32, (1, 128), 1)
 
     lane_bin = lax.broadcasted_iota(jnp.int32, (bins, 128), 1) // 8
@@ -399,16 +419,21 @@
         blocks = tokens // 8
         reach = planes - 1
         deep = planes + 2 * reach
-        smem = pl.BlockSpec(memory_space=pltpu.SMEM)
         vmem = pl.BlockSpec(memory_space=pltpu.VMEM)
         hbm = pl.BlockSpec(memory_space=pl.ANY)
         weights = (phase_qkv, phase_out, window_qkv, window_out, mlp_up, mlp_down)
         result = pl.pallas_call(
             functools.partial(kernel, bins, slabs),
-            out_shape=jax.ShapeDtypeStruct((planes, tokens, width), F32),
-            in_specs=[smem] * 4 + [hbm] * 10,
+            out_shape=pltpu.VMEM((planes, tokens, width), F32),
+            in_specs=[hbm] * 14,
             out_specs=vmem,
-            scratch_shapes=[pltpu.VMEM((1, width), F32)] * 3
+            scratch_shapes=[
+                pltpu.SMEM(bin_phase.shape, jnp.int32),
+                pltpu.SMEM(phase_bias.shape, F32),
+                pltpu.SMEM(window_corner.shape[::-1], jnp.int32),
+                pltpu.SMEM(window_bias.shape, F32),
+            ]
+            + [pltpu.VMEM((1, width), F32)] * 3
             + [pltpu.VMEM(w.shape, BF16) for w in weights]
             + [
                 pltpu.VMEM((planes, blocks, 8, width), BF16),
@@ -419,6 +444,7 @@
                 pltpu.VMEM((deep, tokens, width), BF16),
                 pltpu.VMEM((8, 128, 128), F32),
                 pltpu.VMEM((33, 128, 128), F32),
+                pltpu.SemaphoreType.DMA((4,)),
                 pltpu.SemaphoreType.DMA((9,)),
                 pltpu.SemaphoreType.DMA((3,)),
                 pltpu.SemaphoreType.DMA((8,)),

time: 35.6 us -> 32.8 us (0.921)
  Pallas kernels: 33.6 us -> 32 us
  other arithmetic: 1.77 us -> 0.73 us
    pallas_call x1, Pallas kernels: 33.6 us -> 32 us  [local(): pl.pallas_call(functools.partial(kernel, bins, slabs), out_shape=pltpu.VM...]
    convert_element_type x1, other arithmetic: 1.77 us -> 0.73 us  [local(): return result.astype(BF16).reshape(volume.shape)]
where the time goes in v3:
time: 32.8 us; the launch traced here: 32.7 us
  Pallas kernels  32 us (98%)
  other arithmetic  0.73 us (2%)
    pallas_call x1, Pallas kernels, local(): pl.pallas_call(functools.partial(kernel, bins, slabs), out_shape=pltpu.VM...  32 us
    convert_element_type x1, other arithmetic, local(): return result.astype(BF16).reshape(volume.shape)  0.73 us

profile of v3, /device:TPU:1, one launch (start us, length us, event | category | flops | bytes accessed | tf_op | source)
XLA Modules:
  0.0 32.7 jit_solution(7174885619236795302)
XLA Ops:
  0.0 32.0 %shard_map.136 = f32[4,128,256]{2,1,0:T(8,128)S(1)} custom-call(s32[16]{0:T(128)} %bin_phase_hbm.1, f32[8,16]{1,0:T(8,128)} %phase_bias_hbm.1, s32[3,8]{1,0:T(4,128)} %bitcast.7, f32[8,64]{1,0:T(8,128)} %window_bias_hbm.1, f32[1,256]{1,0:T(1,128)} %bitcast.8, f32[1,256]{1,0:T(1,128)} %bitcast.9, f32[1,256]{1,0:T(1,128)} %bitcast.10, ...), custom_call_target="tpu_custom_call" | custom-call | tf_op jit(solution)/shard_map/pallas_call | solution.py:425
  32.0 0.7 %convert_element_type.3 = bf16[4,128,256]{2,1,0:T(8,128)(2,1)} convert(f32[4,128,256]{2,1,0:T(8,128)S(1)} %shard_map.136) | non-fusion elementwise | flops 131072 | bytes 786432 | tf_op jit(solution)/shard_map/convert_element_type | solution.py:465

commit v4 on v3

--- a/solution.py
+++ b/solution.py
@@ -65,6 +65,7 @@
     queries,
     keys,
     values,
+    attended,
     phase_table,
     window_table,
     table_sem,
@@ -241,6 +242,18 @@
             sent.at[pl.ds(here, half), me], ext.at[pl.ds(reach + here, half), me], local_sem.at[1 + part]
         ).start()
 
+        @pl.loop(1, bins)
+        def _(i):
+            peer = lax.rem(me + i, bins)
+            pltpu.make_async_remote_copy(
+                src_ref=sent.at[pl.ds(here, half), peer],
+                dst_ref=ext.at[pl.ds(reach + here, half), me],
+                send_sem=send_sem.at[2 + part],
+                recv_sem=recv_sem.at[2 + part],
+                device_id={"phase": peer},
+                device_id_type=MESH,
+            ).start()
+
         @pl.when(not_last)
         def _():
             @pl.loop(0, bins)
@@ -269,18 +282,6 @@
                     device_id_type=MESH,
                 ).start()
 
-        @pl.loop(1, bins)
-        def _(i):
-            peer = lax.rem(me + i, bins)
-            pltpu.make_async_remote_copy(
-                src_ref=sent.at[pl.ds(here, half), peer],
-                dst_ref=ext.at[pl.ds(reach + here, half), me],
-                send_sem=send_sem.at[2 + part],
-                recv_sem=recv_sem.at[2 + part],
-                device_id={"phase": peer},
-                device_id_type=MESH,
-            ).start()
-
     def arrived(ref, sem):
         pltpu.make_async_copy(ref, ref, sem).wait()
 
@@ -346,8 +347,7 @@
 
     depth = planes * slabs
 
-    @pl.loop(0, planes)
-    def _(g):
+    def look(g):
         tiles = []
         for t in range(2):
             lanes = slice(128 * t, 128 * t + 128)
@@ -373,11 +373,18 @@
                 top = jnp.where(head_lanes[i], summed[:, :128], top)
                 low = jnp.where(head_lanes[i], summed[:, 128:], low)
             tiles.append((top / low).astype(BF16))
-        mixed = jnp.concatenate(tiles, axis=1)
-        residual = ext[reach + g].astype(F32).reshape(128, 256) + dot(mixed, w_out2[...])
+        attended[g] = jnp.concatenate(tiles, axis=1)
+
+    for g in range(planes):
+        look(g)
+    for part in range(2):
+        here = half * part
+        rows = 128 * half
+        mixed = attended[here : here + half].reshape(rows, 256)
+        residual = ext[reach + here : reach + here + half].astype(F32).reshape(rows, 256) + dot(mixed, w_out2[...])
         hidden = jax.nn.gelu(dot(normed(residual, gain3[...]), w_up[...]), approximate=True)
         final = residual + dot(hidden.astype(BF16), w_down[...])
-        out[g] = final
+        out[here : here + half] = final.reshape(half, 128, 256)
 
     for part in range(2):
         here = half * part
@@ -442,6 +449,7 @@
                 pltpu.VMEM((planes, tokens, width), BF16),
                 pltpu.VMEM((deep, tokens, width), BF16),
                 pltpu.VMEM((deep, tokens, width), BF16),
+                pltpu.VMEM((planes, tokens, width), BF16),
                 pltpu.VMEM((8, 128, 128), F32),
                 pltpu.VMEM((33, 128, 128), F32),
                 pltpu.SemaphoreType.DMA((4,)),

time: 32.8 us -> 30.5 us (0.930)
  Pallas kernels: 32 us -> 29.6 us
    pallas_call x1, Pallas kernels: 32 us -> 29.6 us  [local(): pl.pallas_call(functools.partial(kernel, bins, slabs), out_shape=pltpu.VM...]
where the time goes in v4:
time: 30.5 us; the launch traced here: 30.4 us
  Pallas kernels  29.6 us (97%)
  other arithmetic  0.73 us (2%)
    pallas_call x1, Pallas kernels, local(): pl.pallas_call(functools.partial(kernel, bins, slabs), out_shape=pltpu.VM...  29.6 us
    convert_element_type x1, other arithmetic, local(): return result.astype(BF16).reshape(volume.shape)  0.73 us

profile of v4, /device:TPU:1, one launch (start us, length us, event | category | flops | bytes accessed | tf_op | source)
XLA Modules:
  0.0 30.4 jit_solution(1144884062175485381)
XLA Ops:
  0.0 29.6 %shard_map.136 = f32[4,128,256]{2,1,0:T(8,128)S(1)} custom-call(s32[16]{0:T(128)} %bin_phase_hbm.1, f32[8,16]{1,0:T(8,128)} %phase_bias_hbm.1, s32[3,8]{1,0:T(4,128)} %bitcast.7, f32[8,64]{1,0:T(8,128)} %window_bias_hbm.1, f32[1,256]{1,0:T(1,128)} %bitcast.8, f32[1,256]{1,0:T(1,128)} %bitcast.9, f32[1,256]{1,0:T(1,128)} %bitcast.10, ...), custom_call_target="tpu_custom_call" | custom-call | tf_op jit(solution)/shard_map/pallas_call | solution.py:432
  29.6 0.7 %convert_element_type.3 = bf16[4,128,256]{2,1,0:T(8,128)(2,1)} convert(f32[4,128,256]{2,1,0:T(8,128)S(1)} %shard_map.136) | non-fusion elementwise | flops 131072 | bytes 786432 | tf_op jit(solution)/shard_map/convert_element_type | solution.py:473

commit v5 on v4

--- a/solution.py
+++ b/solution.py
@@ -82,6 +82,7 @@
     unscale = math.sqrt(32)
     rate = scale * math.log2(math.e)
     reach = planes - 1
+    assert planes == 4
     not_first = slab > 0
     not_last = slab < slabs - 1
 
@@ -170,21 +171,24 @@
     sides = not_first.astype(jnp.int32) + not_last.astype(jnp.int32)
     pl.semaphore_wait(barrier, bins - 1 + sides)
 
-    half = planes // 2
-    for part in range(2):
-
+    middle = ((1, 2),)
+    outer = ((0, 1), (3, 1))
+
+    def gather(part, pieces):
         @pl.loop(1, bins)
         def _(i):
             peer = lax.rem(me + i, bins)
-            pltpu.make_async_remote_copy(
-                src_ref=vol.at[pl.ds(half * part, half), peer],
-                dst_ref=got.at[pl.ds(half * part, half), me],
-                send_sem=send_sem.at[part],
-                recv_sem=recv_sem.at[part],
-                device_id={"phase": peer},
-                device_id_type=MESH,
-            ).start()
-
+            for first, count in pieces:
+                pltpu.make_async_remote_copy(
+                    src_ref=vol.at[pl.ds(first, count), peer],
+                    dst_ref=got.at[pl.ds(first, count), me],
+                    send_sem=send_sem.at[part],
+                    recv_sem=recv_sem.at[part],
+                    device_id={"phase": peer},
+                    device_id_type=MESH,
+                ).start()
+
+    gather(0, middle)
     row = lax.broadcasted_iota(jnp.int32, (128, 128), 0)
     column = lax.broadcasted_iota(jnp.int32, (128, 128), 1)
     step_x = column // 32 - row // 32
@@ -203,15 +207,18 @@
                 table = jnp.where(code == j, window_bias[h, 16 * a + j] * unscale, table)
             window_table[4 * h + a] = table
 
+    gather(1, outer)
+
     head_lanes = [(lane // 32) == i for i in range(4)]
     head_keep = [m.astype(F32).astype(BF16) for m in head_lanes]
 
-    def attend(part):
-        rows = 128 * half
-        stream = got[half * part : half * part + half].astype(F32).reshape(rows, 256)
+    def attend(pieces):
+        rows = 256
+        stream = jnp.concatenate([got[f : f + n] for f, n in pieces], axis=0)
+        stream = stream.astype(F32).reshape(rows, 256)
         triple = dot(normed(stream, gain1[...]), w_qkv1[...]).astype(BF16)
         mixed = []
-        for p in range(half):
+        for p in range(2):
             tiles = []
             for t in range(2):
                 q = triple[128 * p : 128 * p + 128, 128 * t : 128 * t + 128]
@@ -231,67 +238,104 @@
                 tiles.append((top / low).astype(BF16))
             mixed.append(jnp.concatenate(tiles, axis=1))
         residual = stream + dot(jnp.concatenate(mixed, axis=0), w_out1[...])
-        sent[half * part : half * part + half] = residual.astype(BF16).reshape(half, blocks, 8, 256)
-
-    def hand_on(part):
-        here = half * part
-        up = max(here, planes - reach)
-        up_count = here + half - up
-        down_count = min(here + half, reach) - here
-        pltpu.make_async_copy(
-            sent.at[pl.ds(here, half), me], ext.at[pl.ds(reach + here, half), me], local_sem.at[1 + part]
-        ).start()
+        residual = residual.astype(BF16).reshape(2, blocks, 8, 256)
+        at = 0
+        for f, n in pieces:
+            sent[f : f + n] = residual[at : at + n]
+            at += n
+
+    even = lax.rem(slab, 2) == 0
+    low, high = 0, reach + planes
+    partner = jnp.where(even, slab + 1, slab - 1)
+    partner_slot = jnp.where(even, low, high + 1)
+    held_slot = jnp.where(even, high + 1, low)
+    onward = jnp.where(even, slab + 2, slab - 2)
+    sends_on = (onward >= 0) & (onward < slabs)
+    taken_from = jnp.where(even, slab - 2, slab + 2)
+    takes = (taken_from >= 0) & (taken_from < slabs)
+
+    def to_owner(part, pieces):
+        for first, count in pieces:
+            pltpu.make_async_copy(
+                sent.at[pl.ds(first, count), me],
+                ext.at[pl.ds(reach + first, count), me],
+                local_sem.at[1 + part],
+            ).start()
 
         @pl.loop(1, bins)
         def _(i):
             peer = lax.rem(me + i, bins)
+            for first, count in pieces:
+                pltpu.make_async_remote_copy(
+                    src_ref=sent.at[pl.ds(first, count), peer],
+                    dst_ref=ext.at[pl.ds(reach + first, count), me],
+                    send_sem=send_sem.at[2 + part],
+                    recv_sem=recv_sem.at[2 + part],
+                    device_id={"phase": peer},
+                    device_id_type=MESH,
+                ).start()
+
+    def to_slab(first, count, slot, target, sem):
+        @pl.loop(0, bins)
+        def _(i):
+            peer = lax.rem(me + i, bins)
             pltpu.make_async_remote_copy(
-                src_ref=sent.at[pl.ds(here, half), peer],
-                dst_ref=ext.at[pl.ds(reach + here, half), me],
-                send_sem=send_sem.at[2 + part],
-                recv_sem=recv_sem.at[2 + part],
-                device_id={"phase": peer},
+                src_ref=sent.at[pl.ds(first, count), peer],
+                dst_ref=ext.at[pl.ds(slot, count), me],
+                send_sem=send_sem.at[sem],
+                recv_sem=recv_sem.at[sem],
+                device_id={"phase": peer, "space": target},
                 device_id_type=MESH,
             ).start()
 
-        @pl.when(not_last)
-        def _():
-            @pl.loop(0, bins)
-            def _(i):
-                peer = lax.rem(me + i, bins)
-                pltpu.make_async_remote_copy(
-                    src_ref=sent.at[pl.ds(up, up_count), peer],
-                    dst_ref=ext.at[pl.ds(up - (planes - reach), up_count), me],
-                    send_sem=send_sem.at[4 + part],
-                    recv_sem=recv_sem.at[4 + part],
-                    device_id={"phase": peer, "space": slab + 1},
-                    device_id_type=MESH,
-                ).start()
-
-        @pl.when(not_first)
-        def _():
-            @pl.loop(0, bins)
-            def _(i):
-                peer = lax.rem(me + i, bins)
-                pltpu.make_async_remote_copy(
-                    src_ref=sent.at[pl.ds(here, down_count), peer],
-                    dst_ref=ext.at[pl.ds(reach + planes + here, down_count), me],
-                    send_sem=send_sem.at[6 + part],
-                    recv_sem=recv_sem.at[6 + part],
-                    device_id={"phase": peer, "space": slab - 1},
-                    device_id_type=MESH,
-                ).start()
-
     def arrived(ref, sem):
         pltpu.make_async_copy(ref, ref, sem).wait()
+
+    two_blocks = got.at[pl.ds(0, 2), pl.ds(0, bins - 1)]
+
+    def owned(part, pieces):
+        for first, count in pieces:
+            pltpu.make_async_copy(
+                sent.at[pl.ds(first, count), me],
+                ext.at[pl.ds(reach + first, count), me],
+                local_sem.at[1 + part],
+            ).wait()
+        arrived(two_blocks, recv_sem.at[2 + part])
 
     own_in.wait()
     for copy in weight_copies[:3]:
         copy.wait()
-    for part in range(2):
-        arrived(got.at[pl.ds(0, half), pl.ds(0, bins - 1)], recv_sem.at[part])
-        attend(part)
-        hand_on(part)
+    arrived(two_blocks, recv_sem.at[0])
+    attend(middle)
+    to_slab(1, 2, partner_slot, partner, 4)
+    to_owner(0, middle)
+    arrived(two_blocks, recv_sem.at[1])
+    attend(outer)
+    @pl.when(not_last)
+    def _():
+        to_slab(3, 1, low + reach - 1, slab + 1, 5)
+
+    @pl.when(not_first)
+    def _():
+        to_slab(0, 1, high, slab - 1, 6)
+
+    to_owner(1, outer)
+
+    def forward():
+        return pltpu.make_async_remote_copy(
+            src_ref=ext.at[pl.ds(held_slot, 2)],
+            dst_ref=ext.at[pl.ds(partner_slot, 2)],
+            send_sem=send_sem.at[7],
+            recv_sem=recv_sem.at[7],
+            device_id={"space": onward},
+            device_id_type=MESH,
+        )
+
+    arrived(ext.at[pl.ds(0, 2)], recv_sem.at[4])
+
+    @pl.when(sends_on)
+    def _():
+        forward().start()
 
     for copy in weight_copies[3:5]:
         copy.wait()
@@ -308,39 +352,32 @@
             keys[plane] = triple[:, 256:512]
             values[plane] = triple[:, 512:]
 
-    for part in range(2):
-        pltpu.make_async_copy(
-            sent.at[pl.ds(0, half), me], ext.at[pl.ds(reach, half), me], local_sem.at[1 + part]
-        ).wait()
-        arrived(got.at[pl.ds(0, half), pl.ds(0, bins - 1)], recv_sem.at[2 + part])
-
-        @pl.loop(half * part, half * part + half)
-        def _(g):
-            project(reach + g, g)
-
-    for part in range(2):
-        here = half * part
-        up = max(here, planes - reach)
-        up_count = here + half - up
-        down_count = min(here + half, reach) - here
-
-        @pl.when(not_first)
-        def _():
-            arrived(ext.at[pl.ds(0, up_count)], recv_sem.at[4 + part])
-
-        @pl.when(not_last)
-        def _():
-            arrived(ext.at[pl.ds(0, down_count)], recv_sem.at[6 + part])
-
-        first = up - (planes - reach)
-
-        @pl.loop(first, first + up_count)
-        def _(g):
-            project(g, None)
-
-        @pl.loop(reach + planes + here, reach + planes + here + down_count)
-        def _(g):
-            project(g, None)
+    for i in range(2):
+        project(held_slot + i, None)
+    owned(0, middle)
+    for g in (1, 2):
+        project(reach + g, g)
+    owned(1, outer)
+    for g in (0, 3):
+        project(reach + g, g)
+
+    @pl.when(not_first)
+    def _():
+        arrived(ext.at[pl.ds(0, 1)], recv_sem.at[5])
+
+    @pl.when(not_last)
+    def _():
+        arrived(ext.at[pl.ds(0, 1)], recv_sem.at[6])
+
+    for slot in (low + reach - 1, high):
+        project(slot, None)
+
+    @pl.when(takes)
+    def _():
+        arrived(ext.at[pl.ds(0, 2)], recv_sem.at[7])
+
+    for i in range(2):
+        project(partner_slot + i, None)
 
     for copy in weight_copies[5:]:
         copy.wait()
@@ -377,6 +414,7 @@
 
     for g in range(planes):
         look(g)
+    half = planes // 2
     for part in range(2):
         here = half * part
         rows = 128 * half
@@ -386,20 +424,21 @@
         final = residual + dot(hidden.astype(BF16), w_down[...])
         out[here : here + half] = final.reshape(half, 128, 256)
 
-    for part in range(2):
-        here = half * part
-        up_count = here + half - max(here, planes - reach)
-        down_count = min(here + half, reach) - here
-        arrived(got.at[pl.ds(0, half), pl.ds(0, bins - 1)], send_sem.at[part])
-        arrived(got.at[pl.ds(0, half), pl.ds(0, bins - 1)], send_sem.at[2 + part])
-
-        @pl.when(not_last)
-        def _():
-            arrived(ext.at[pl.ds(0, up_count)], send_sem.at[4 + part])
-
-        @pl.when(not_first)
-        def _():
-            arrived(ext.at[pl.ds(0, down_count)], send_sem.at[6 + part])
+    for sem in range(4):
+        arrived(two_blocks, send_sem.at[sem])
+    arrived(ext.at[pl.ds(0, 2)], send_sem.at[4])
+
+    @pl.when(not_last)
+    def _():
+        arrived(ext.at[pl.ds(0, 1)], send_sem.at[5])
+
+    @pl.when(not_first)
+    def _():
+        arrived(ext.at[pl.ds(0, 1)], send_sem.at[6])
+
+    @pl.when(sends_on)
+    def _():
+        forward().wait_send()
 
 
 def solution(mesh):

time: 30.5 us -> 26.4 us (0.87)
  Pallas kernels: 29.6 us -> 25.5 us
    pallas_call x1, Pallas kernels: 29.6 us -> 25.5 us  [local(): pl.pallas_call(functools.partial(kernel, bins, slabs), out_shape=pltpu.VM...]
where the time goes in v5:
time: 26.4 us; the launch traced here: 26.2 us
  Pallas kernels  25.5 us (97%)
  other arithmetic  0.73 us (3%)
    pallas_call x1, Pallas kernels, local(): pl.pallas_call(functools.partial(kernel, bins, slabs), out_shape=pltpu.VM...  25.5 us
    convert_element_type x1, other arithmetic, local(): return result.astype(BF16).reshape(volume.shape)  0.73 us

profile of v5, /device:TPU:1, one launch (start us, length us, event | category | flops | bytes accessed | tf_op | source)
XLA Modules:
  0.0 26.2 jit_solution(8708248985874781745)
XLA Ops:
  0.0 25.5 %shard_map.136 = f32[4,128,256]{2,1,0:T(8,128)S(1)} custom-call(s32[16]{0:T(128)} %bin_phase_hbm.1, f32[8,16]{1,0:T(8,128)} %phase_bias_hbm.1, s32[3,8]{1,0:T(4,128)} %bitcast.7, f32[8,64]{1,0:T(8,128)} %window_bias_hbm.1, f32[1,256]{1,0:T(1,128)} %bitcast.8, f32[1,256]{1,0:T(1,128)} %bitcast.9, f32[1,256]{1,0:T(1,128)} %bitcast.10, ...), custom_call_target="tpu_custom_call" | custom-call | tf_op jit(solution)/shard_map/pallas_call | solution.py:471
  25.5 0.7 %convert_element_type.3 = bf16[4,128,256]{2,1,0:T(8,128)(2,1)} convert(f32[4,128,256]{2,1,0:T(8,128)S(1)} %shard_map.136) | non-fusion elementwise | flops 131072 | bytes 786432 | tf_op jit(solution)/shard_map/convert_element_type | solution.py:512

commit v6 on v5

--- a/solution.py
+++ b/solution.py
@@ -71,6 +71,7 @@
     table_sem,
     weight_sem,
     local_sem,
+    own_sem,
     send_sem,
     recv_sem,
 ):
@@ -171,24 +172,21 @@
     sides = not_first.astype(jnp.int32) + not_last.astype(jnp.int32)
     pl.semaphore_wait(barrier, bins - 1 + sides)
 
-    middle = ((1, 2),)
-    outer = ((0, 1), (3, 1))
-
-    def gather(part, pieces):
+    def gather(plane):
         @pl.loop(1, bins)
         def _(i):
             peer = lax.rem(me + i, bins)
-            for first, count in pieces:
-                pltpu.make_async_remote_copy(
-                    src_ref=vol.at[pl.ds(first, count), peer],
-                    dst_ref=got.at[pl.ds(first, count), me],
-                    send_sem=send_sem.at[part],
-                    recv_sem=recv_sem.at[part],
-                    device_id={"phase": peer},
-                    device_id_type=MESH,
-                ).start()
-
-    gather(0, middle)
+            pltpu.make_async_remote_copy(
+                src_ref=vol.at[plane, peer],
+                dst_ref=got.at[plane, me],
+                send_sem=send_sem.at[plane],
+                recv_sem=recv_sem.at[plane],
+                device_id={"phase": peer},
+                device_id_type=MESH,
+            ).start()
+
+    gather(1)
+    gather(2)
     row = lax.broadcasted_iota(jnp.int32, (128, 128), 0)
     column = lax.broadcasted_iota(jnp.int32, (128, 128), 1)
     step_x = column // 32 - row // 32
@@ -207,18 +205,17 @@
                 table = jnp.where(code == j, window_bias[h, 16 * a + j] * unscale, table)
             window_table[4 * h + a] = table
 
-    gather(1, outer)
+    gather(0)
+    gather(3)
 
     head_lanes = [(lane // 32) == i for i in range(4)]
     head_keep = [m.astype(F32).astype(BF16) for m in head_lanes]
 
-    def attend(pieces):
-        rows = 256
-        stream = jnp.concatenate([got[f : f + n] for f, n in pieces], axis=0)
-        stream = stream.astype(F32).reshape(rows, 256)
+    def attend(plane):
+        stream = got[plane].astype(F32).reshape(128, 256)
         triple = dot(normed(stream, gain1[...]), w_qkv1[...]).astype(BF16)
         mixed = []
-        for p in range(2):
+        for p in range(1):
             tiles = []
             for t in range(2):
                 q = triple[128 * p : 128 * p + 128, 128 * t : 128 * t + 128]
@@ -238,11 +235,7 @@
                 tiles.append((top / low).astype(BF16))
             mixed.append(jnp.concatenate(tiles, axis=1))
         residual = stream + dot(jnp.concatenate(mixed, axis=0), w_out1[...])
-        residual = residual.astype(BF16).reshape(2, blocks, 8, 256)
-        at = 0
-        for f, n in pieces:
-            sent[f : f + n] = residual[at : at + n]
-            at += n
+        sent[plane] = residual.astype(BF16).reshape(blocks, 8, 256)
 
     even = lax.rem(slab, 2) == 0
     low, high = 0, reach + planes
@@ -254,34 +247,30 @@
     taken_from = jnp.where(even, slab - 2, slab + 2)
     takes = (taken_from >= 0) & (taken_from < slabs)
 
-    def to_owner(part, pieces):
-        for first, count in pieces:
-            pltpu.make_async_copy(
-                sent.at[pl.ds(first, count), me],
-                ext.at[pl.ds(reach + first, count), me],
-                local_sem.at[1 + part],
-            ).start()
+    def to_owner(plane):
+        pltpu.make_async_copy(
+            sent.at[plane, me], ext.at[reach + plane, me], own_sem.at[plane]
+        ).start()
 
         @pl.loop(1, bins)
         def _(i):
             peer = lax.rem(me + i, bins)
-            for first, count in pieces:
-                pltpu.make_async_remote_copy(
-                    src_ref=sent.at[pl.ds(first, count), peer],
-                    dst_ref=ext.at[pl.ds(reach + first, count), me],
-                    send_sem=send_sem.at[2 + part],
-                    recv_sem=recv_sem.at[2 + part],
-                    device_id={"phase": peer},
-                    device_id_type=MESH,
-                ).start()
-
-    def to_slab(first, count, slot, target, sem):
+            pltpu.make_async_remote_copy(
+                src_ref=sent.at[plane, peer],
+                dst_ref=ext.at[reach + plane, me],
+                send_sem=send_sem.at[4 + plane],
+                recv_sem=recv_sem.at[4 + plane],
+                device_id={"phase": peer},
+                device_id_type=MESH,
+            ).start()
+
+    def to_slab(plane, slot, target, sem):
         @pl.loop(0, bins)
         def _(i):
             peer = lax.rem(me + i, bins)
             pltpu.make_async_remote_copy(
-                src_ref=sent.at[pl.ds(first, count), peer],
-                dst_ref=ext.at[pl.ds(slot, count), me],
+                src_ref=sent.at[plane, peer],
+                dst_ref=ext.at[slot, me],
                 send_sem=send_sem.at[sem],
                 recv_sem=recv_sem.at[sem],
                 device_id={"phase": peer, "space": target},
@@ -291,51 +280,53 @@
     def arrived(ref, sem):
         pltpu.make_async_copy(ref, ref, sem).wait()
 
-    two_blocks = got.at[pl.ds(0, 2), pl.ds(0, bins - 1)]
-
-    def owned(part, pieces):
-        for first, count in pieces:
-            pltpu.make_async_copy(
-                sent.at[pl.ds(first, count), me],
-                ext.at[pl.ds(reach + first, count), me],
-                local_sem.at[1 + part],
-            ).wait()
-        arrived(two_blocks, recv_sem.at[2 + part])
+    others = got.at[0, pl.ds(0, bins - 1)]
+
+    def owned(plane):
+        pltpu.make_async_copy(
+            sent.at[plane, me], ext.at[reach + plane, me], own_sem.at[plane]
+        ).wait()
+        arrived(others, recv_sem.at[4 + plane])
 
     own_in.wait()
     for copy in weight_copies[:3]:
         copy.wait()
-    arrived(two_blocks, recv_sem.at[0])
-    attend(middle)
-    to_slab(1, 2, partner_slot, partner, 4)
-    to_owner(0, middle)
-    arrived(two_blocks, recv_sem.at[1])
-    attend(outer)
+    for plane in (1, 2):
+        arrived(others, recv_sem.at[plane])
+        attend(plane)
+        to_slab(plane, partner_slot + plane - 1, partner, 7 + plane)
+        to_owner(plane)
+    arrived(others, recv_sem.at[0])
+    attend(0)
+    @pl.when(not_first)
+    def _():
+        to_slab(0, high, slab - 1, 10)
+
+    to_owner(0)
+    arrived(others, recv_sem.at[3])
+    attend(3)
     @pl.when(not_last)
     def _():
-        to_slab(3, 1, low + reach - 1, slab + 1, 5)
-
-    @pl.when(not_first)
-    def _():
-        to_slab(0, 1, high, slab - 1, 6)
-
-    to_owner(1, outer)
-
-    def forward():
+        to_slab(3, low + reach - 1, slab + 1, 11)
+
+    to_owner(3)
+
+    def forward(i):
         return pltpu.make_async_remote_copy(
-            src_ref=ext.at[pl.ds(held_slot, 2)],
-            dst_ref=ext.at[pl.ds(partner_slot, 2)],
-            send_sem=send_sem.at[7],
-            recv_sem=recv_sem.at[7],
+            src_ref=ext.at[held_slot + i],
+            dst_ref=ext.at[partner_slot + i],
+            send_sem=send_sem.at[12 + i],
+            recv_sem=recv_sem.at[12 + i],
             device_id={"space": onward},
             device_id_type=MESH,
         )
 
-    arrived(ext.at[pl.ds(0, 2)], recv_sem.at[4])
-
-    @pl.when(sends_on)
-    def _():
-        forward().start()
+    for i in range(2):
+        arrived(ext.at[0], recv_sem.at[8 + i])
+
+        @pl.when(sends_on)
+        def _():
+            forward(i).start()
 
     for copy in weight_copies[3:5]:
         copy.wait()
@@ -354,27 +345,30 @@
 
     for i in range(2):
         project(held_slot + i, None)
-    owned(0, middle)
+    owned(1)
+    owned(2)
     for g in (1, 2):
         project(reach + g, g)
-    owned(1, outer)
+    owned(0)
+    owned(3)
     for g in (0, 3):
         project(reach + g, g)
 
     @pl.when(not_first)
     def _():
-        arrived(ext.at[pl.ds(0, 1)], recv_sem.at[5])
+        arrived(ext.at[0], recv_sem.at[11])
 
     @pl.when(not_last)
     def _():
-        arrived(ext.at[pl.ds(0, 1)], recv_sem.at[6])
+        arrived(ext.at[0], recv_sem.at[10])
 
     for slot in (low + reach - 1, high):
         project(slot, None)
 
     @pl.when(takes)
     def _():
-        arrived(ext.at[pl.ds(0, 2)], recv_sem.at[7])
+        arrived(ext.at[0], recv_sem.at[12])
+        arrived(ext.at[0], recv_sem.at[13])
 
     for i in range(2):
         project(partner_slot + i, None)
@@ -420,25 +414,31 @@
         rows = 128 * half
         mixed = attended[here : here + half].reshape(rows, 256)
         residual = ext[reach + here : reach + here + half].astype(F32).reshape(rows, 256) + dot(mixed, w_out2[...])
-        hidden = jax.nn.gelu(dot(normed(residual, gain3[...]), w_up[...]), approximate=True)
+        rise = dot(normed(residual, gain3[...]), w_up[...])
+        slope = math.sqrt(2.0 / math.pi)
+        bend = jnp.tanh(rise * (slope + (0.044715 * slope) * (rise * rise)))
+        level = 0.5 * rise
+        hidden = level + level * bend
         final = residual + dot(hidden.astype(BF16), w_down[...])
         out[here : here + half] = final.reshape(half, 128, 256)
 
-    for sem in range(4):
-        arrived(two_blocks, send_sem.at[sem])
-    arrived(ext.at[pl.ds(0, 2)], send_sem.at[4])
+    for sem in range(8):
+        arrived(others, send_sem.at[sem])
+    for sem in (8, 9):
+        arrived(ext.at[0], send_sem.at[sem])
+
+    @pl.when(not_first)
+    def _():
+        arrived(ext.at[0], send_sem.at[10])
 
     @pl.when(not_last)
     def _():
-        arrived(ext.at[pl.ds(0, 1)], send_sem.at[5])
-
-    @pl.when(not_first)
-    def _():
-        arrived(ext.at[pl.ds(0, 1)], send_sem.at[6])
+        arrived(ext.at[0], send_sem.at[11])
 
     @pl.when(sends_on)
     def _():
-        forward().wait_send()
+        forward(0).wait_send()
+        forward(1).wait_send()
 
 
 def solution(mesh):
@@ -493,9 +493,10 @@
                 pltpu.VMEM((33, 128, 128), F32),
                 pltpu.SemaphoreType.DMA((4,)),
                 pltpu.SemaphoreType.DMA((9,)),
-                pltpu.SemaphoreType.DMA((3,)),
-                pltpu.SemaphoreType.DMA((8,)),
-                pltpu.SemaphoreType.DMA((8,)),
+                pltpu.SemaphoreType.DMA((4,)),
+                pltpu.SemaphoreType.DMA((4,)),
+                pltpu.SemaphoreType.DMA((14,)),
+                pltpu.SemaphoreType.DMA((14,)),
             ],
             compiler_params=pltpu.CompilerParams(collective_id=0, has_side_effects=True),
         )(

time: 26.4 us -> 26 us (0.985)
  the two profiles are of different devices: /device:TPU:1 before, /device:TPU:96 now
where the time goes in v6:
time: 26 us; the launch traced here: 25.9 us
  Pallas kernels  25.1 us (97%)
  other arithmetic  0.73 us (3%)
    pallas_call x1, Pallas kernels, local(): pl.pallas_call(functools.partial(kernel, bins, slabs), out_shape=pltpu.VM...  25.1 us
    convert_element_type x1, other arithmetic, local(): return result.astype(BF16).reshape(volume.shape)  0.73 us

profile of v6, /device:TPU:96, one launch (start us, length us, event | category | flops | bytes accessed | tf_op | source)
XLA Modules:
  0.0 25.9 jit_solution(6704130199024014815)
XLA Ops:
  0.0 25.1 %shard_map.136 = f32[4,128,256]{2,1,0:T(8,128)S(1)} custom-call(s32[16]{0:T(128)} %bin_phase_hbm.1, f32[8,16]{1,0:T(8,128)} %phase_bias_hbm.1, s32[3,8]{1,0:T(4,128)} %bitcast.7, f32[8,64]{1,0:T(8,128)} %window_bias_hbm.1, f32[1,256]{1,0:T(1,128)} %bitcast.8, f32[1,256]{1,0:T(1,128)} %bitcast.9, f32[1,256]{1,0:T(1,128)} %bitcast.10, ...), custom_call_target="tpu_custom_call" | custom-call | tf_op jit(solution)/shard_map/pallas_call | solution.py:471
  25.1 0.7 %convert_element_type.3 = bf16[4,128,256]{2,1,0:T(8,128)(2,1)} convert(f32[4,128,256]{2,1,0:T(8,128)S(1)} %shard_map.136) | non-fusion elementwise | flops 131072 | bytes 786432 | tf_op jit(solution)/shard_map/convert_element_type | solution.py:513

commit v7 on v6

--- a/solution.py
+++ b/solution.py
@@ -65,9 +65,11 @@
     queries,
     keys,
     values,
-    attended,
     phase_table,
     window_table,
+    tops,
+    lows,
+    highs,
     table_sem,
     weight_sem,
     local_sem,
@@ -187,11 +189,13 @@
 
     gather(1)
     gather(2)
-    row = lax.broadcasted_iota(jnp.int32, (128, 128), 0)
-    column = lax.broadcasted_iota(jnp.int32, (128, 128), 1)
-    step_x = column // 32 - row // 32
-    step_y = column % 32 - row % 32
-    window_table[4 * heads] = jnp.full((128, 128), MASKED, F32)
+    row = lax.broadcasted_iota(jnp.int32, (32, 128), 0)
+    column = lax.broadcasted_iota(jnp.int32, (32, 128), 1)
+    key = lax.rem(column, 64)
+    step_x = key // 16 - row // 8
+    step_y = lax.rem(key, 16) - lax.rem(row, 8) - 4
+    one_end = (lax.rem(row, 8) < 4) == (lax.rem(key, 16) < 8)
+    masked = jnp.full((32, 128), MASKED, F32)
 
     @pl.loop(0, heads)
     def _(h):
@@ -199,11 +203,19 @@
         c = step_y - corner[2, h]
         inside = (b >= 0) & (b < 4) & (c >= 0) & (c < 4)
         code = jnp.where(inside, 4 * b + c, 16)
+        steps = []
         for a in range(4):
-            table = jnp.full((128, 128), MASKED, F32)
+            table = masked
             for j in range(16):
                 table = jnp.where(code == j, window_bias[h, 16 * a + j] * unscale, table)
-            window_table[4 * h + a] = table
+            steps.append(table)
+        for ends in range(2):
+            sides = [jnp.where(one_end, table, MASKED) if ends else table for table in steps] + [masked]
+            for left in range(5):
+                for right in range(5):
+                    window_table[2 * h + ends, 5 * left + right] = jnp.where(
+                        column < 64, sides[left], sides[right]
+                    )
 
     gather(0)
     gather(3)
@@ -252,8 +264,7 @@
             sent.at[plane, me], ext.at[reach + plane, me], own_sem.at[plane]
         ).start()
 
-        @pl.loop(1, bins)
-        def _(i):
+        for i in range(1, bins):
             peer = lax.rem(me + i, bins)
             pltpu.make_async_remote_copy(
                 src_ref=sent.at[plane, peer],
@@ -265,8 +276,7 @@
             ).start()
 
     def to_slab(plane, slot, target, sem):
-        @pl.loop(0, bins)
-        def _(i):
+        for i in range(bins):
             peer = lax.rem(me + i, bins)
             pltpu.make_async_remote_copy(
                 src_ref=sent.at[plane, peer],
@@ -291,25 +301,28 @@
     own_in.wait()
     for copy in weight_copies[:3]:
         copy.wait()
-    for plane in (1, 2):
-        arrived(others, recv_sem.at[plane])
-        attend(plane)
-        to_slab(plane, partner_slot + plane - 1, partner, 7 + plane)
-        to_owner(plane)
+    arrived(others, recv_sem.at[1])
+    attend(1)
+    arrived(others, recv_sem.at[2])
+    to_slab(1, partner_slot, partner, 8)
+    to_owner(1)
+    attend(2)
     arrived(others, recv_sem.at[0])
+    to_slab(2, partner_slot + 1, partner, 9)
+    to_owner(2)
     attend(0)
+    arrived(others, recv_sem.at[3])
+    to_owner(0)
+    attend(3)
+    to_owner(3)
+
     @pl.when(not_first)
     def _():
         to_slab(0, high, slab - 1, 10)
 
-    to_owner(0)
-    arrived(others, recv_sem.at[3])
-    attend(3)
     @pl.when(not_last)
     def _():
         to_slab(3, low + reach - 1, slab + 1, 11)
-
-    to_owner(3)
 
     def forward(i):
         return pltpu.make_async_remote_copy(
@@ -321,6 +334,96 @@
             device_id_type=MESH,
         )
 
+    for copy in weight_copies[3:5]:
+        copy.wait()
+
+    def banded(target, plane, rows):
+        blocked = rows.reshape(4, 4, 8, 256)
+        for b in range(4):
+            near = blocked[:, b : b + 1]
+            far = blocked[:, (b + 1) % 4 : (b + 1) % 4 + 1]
+            target[plane, b] = jnp.concatenate([near, far], axis=1).reshape(64, 256).astype(BF16)
+
+    def project(plane, inner):
+        stream = ext[plane].astype(F32).reshape(128, 256)
+        if inner is None:
+            pair = dot(normed(stream, gain2[...]), w_qkv2[:, 256:])
+        else:
+            triple = dot(normed(stream, gain2[...]), w_qkv2[...])
+            turned = [pltpu.roll(triple[32 * x : 32 * x + 32, :256], 28, 0) for x in range(4)]
+            for b in range(4):
+                queries[inner, 32 * b : 32 * b + 32] = jnp.concatenate(
+                    [turned[x][8 * b : 8 * b + 8] for x in range(4)], axis=0
+                ).astype(BF16)
+            pair = triple[:, 256:]
+        banded(keys, plane, pair[:, :256])
+        banded(values, plane, pair[:, 256:])
+
+    depth = planes * slabs
+
+    def entries(query_planes, key_planes):
+        found = []
+        for h in range(heads):
+            rows = []
+            for g in query_planes:
+                steps = []
+                for k in key_planes:
+                    a = k - g - corner[0, h]
+                    z = slab * planes + k
+                    usable = (a >= 0) & (a < 4) & (z >= 0) & (z < depth)
+                    steps.append(jnp.where(usable, a, 4))
+                rows.append([5 * steps[j] + steps[j + 1] for j in range(0, len(steps), 2)])
+            found.append(rows)
+        return found
+
+    def look(query_planes, key_planes, merge):
+        entry = entries(query_planes, key_planes)
+        count = len(query_planes)
+        size = 32 * count
+        for t in range(2):
+            lanes = slice(128 * t, 128 * t + 128)
+            for b in range(4):
+                q = jnp.concatenate([queries[g, 32 * b : 32 * b + 32, lanes] for g in query_planes], axis=0)
+                stacked = jnp.concatenate([q * keep for keep in head_keep], axis=0)
+                k = jnp.concatenate([keys[p + reach, b, :, lanes] for p in key_planes], axis=0)
+                v = jnp.concatenate([values[p + reach, b, :, lanes] for p in key_planes], axis=0)
+                both = jnp.concatenate([v, jnp.ones(v.shape, BF16)], axis=1)
+                table = jnp.concatenate(
+                    [
+                        jnp.concatenate([window_table[2 * h + b // 3, e] for e in rows], axis=1)
+                        for h in range(4 * t, 4 * t + 4)
+                        for rows in entry[h]
+                    ],
+                    axis=0,
+                )
+                z = dot_t(stacked, k) + table
+                peak = jnp.max(z, axis=1, keepdims=True)
+                weight = jnp.exp2((z - peak) * rate).astype(BF16)
+                summed = dot(weight, both)
+                top = summed[:size, :128]
+                low = summed[:size, 128:]
+                high = jnp.broadcast_to(peak[:size], (size, 128))
+                for i in range(1, 4):
+                    part = slice(size * i, size * i + size)
+                    top = jnp.where(head_lanes[i], summed[part, :128], top)
+                    low = jnp.where(head_lanes[i], summed[part, 128:], low)
+                    high = jnp.where(head_lanes[i], peak[part], high)
+                top = top.reshape(count, 32, 128)
+                low = low.reshape(count, 32, 128)
+                high = high.reshape(count, 32, 128)
+                at = (t, b, pl.ds(query_planes[0], count))
+                if merge:
+                    before = highs[at]
+                    peak = jnp.maximum(before, high)
+                    old = jnp.exp2((before - peak) * rate)
+                    new = jnp.exp2((high - peak) * rate)
+                    top = tops[at] * old + top * new
+                    low = lows[at] * old + low * new
+                    high = peak
+                tops[at] = top
+                lows[at] = low
+                highs[at] = high
+
     for i in range(2):
         arrived(ext.at[0], recv_sem.at[8 + i])
 
@@ -328,32 +431,16 @@
         def _():
             forward(i).start()
 
-    for copy in weight_copies[3:5]:
-        copy.wait()
-
-    def project(plane, inner):
-        stream = ext[plane].astype(F32).reshape(128, 256)
-        if inner is None:
-            pair = dot(normed(stream, gain2[...]), w_qkv2[:, 256:]).astype(BF16)
-            keys[plane] = pair[:, :256]
-            values[plane] = pair[:, 256:]
-        else:
-            triple = dot(normed(stream, gain2[...]), w_qkv2[...]).astype(BF16)
-            queries[inner] = triple[:, :256]
-            keys[plane] = triple[:, 256:512]
-            values[plane] = triple[:, 512:]
-
-    for i in range(2):
+        owned(1 + i)
         project(held_slot + i, None)
-    owned(1)
-    owned(2)
-    for g in (1, 2):
-        project(reach + g, g)
+        project(reach + 1 + i, 1 + i)
     owned(0)
     owned(3)
     for g in (0, 3):
         project(reach + g, g)
 
+    look(range(planes), range(planes), False)
+
     @pl.when(not_first)
     def _():
         arrived(ext.at[0], recv_sem.at[11])
@@ -365,62 +452,46 @@
     for slot in (low + reach - 1, high):
         project(slot, None)
 
-    @pl.when(takes)
-    def _():
-        arrived(ext.at[0], recv_sem.at[12])
-        arrived(ext.at[0], recv_sem.at[13])
-
-    for i in range(2):
-        project(partner_slot + i, None)
-
+    ahead = jnp.where(even, 2, 0)
+    behind = 2 - ahead
+    look([ahead, ahead + 1], [held_slot - reach, held_slot - reach + 1, -1, planes], True)
     for copy in weight_copies[5:]:
         copy.wait()
 
-    depth = planes * slabs
-
-    def look(g):
-        tiles = []
-        for t in range(2):
-            lanes = slice(128 * t, 128 * t + 128)
-            q = queries[g, :, lanes]
-            top = jnp.zeros((128, 128), F32)
-            low = jnp.ones((128, 128), F32)
-            for i in range(4):
-                h = 4 * t + i
-                low_z = g + corner[0, h]
-                first = low_z + reach
-                k = keys[pl.ds(first, 4), :, lanes].reshape(512, 128)
-                v = values[pl.ds(first, 4), :, lanes].reshape(512, 128)
-                parts = []
-                for a in range(4):
-                    z_key = slab * planes + low_z + a
-                    outside = (z_key < 0) | (z_key >= depth)
-                    parts.append(window_table[jnp.where(outside, 4 * heads, 4 * h + a)])
-                z = dot_t(q * head_keep[i], k) + jnp.concatenate(parts, axis=1)
-                peak = jnp.max(z, axis=1, keepdims=True)
-                weight = jnp.exp2((z - peak) * rate).astype(BF16)
-                both = jnp.concatenate([v, jnp.ones((512, 128), BF16)], axis=1)
-                summed = dot(weight, both)
-                top = jnp.where(head_lanes[i], summed[:, :128], top)
-                low = jnp.where(head_lanes[i], summed[:, 128:], low)
-            tiles.append((top / low).astype(BF16))
-        attended[g] = jnp.concatenate(tiles, axis=1)
-
-    for g in range(planes):
-        look(g)
-    half = planes // 2
-    for part in range(2):
-        here = half * part
-        rows = 128 * half
-        mixed = attended[here : here + half].reshape(rows, 256)
-        residual = ext[reach + here : reach + here + half].astype(F32).reshape(rows, 256) + dot(mixed, w_out2[...])
+    def finish(first):
+        rows = []
+        for j in range(2):
+            tiles = []
+            for t in range(2):
+                share = [tops[t, b, first + j] / lows[t, b, first + j] for b in range(4)]
+                turned = [
+                    jnp.concatenate([share[b][8 * x : 8 * x + 8] for b in range(4)], axis=0) for x in range(4)
+                ]
+                tiles.append(jnp.concatenate([pltpu.roll(part, 4, 0) for part in turned], axis=0))
+            rows.append(jnp.concatenate(tiles, axis=1))
+        mixed = jnp.concatenate(rows, axis=0).astype(BF16)
+        stream = ext[pl.ds(reach + first, 2)].astype(F32).reshape(256, 256)
+        residual = stream + dot(mixed, w_out2[...])
         rise = dot(normed(residual, gain3[...]), w_up[...])
         slope = math.sqrt(2.0 / math.pi)
         bend = jnp.tanh(rise * (slope + (0.044715 * slope) * (rise * rise)))
         level = 0.5 * rise
         hidden = level + level * bend
         final = residual + dot(hidden.astype(BF16), w_down[...])
-        out[here : here + half] = final.reshape(half, 128, 256)
+        out[pl.ds(first, 2)] = final.reshape(2, 128, 256)
+
+
+    @pl.when(takes)
+    def _():
+        arrived(ext.at[0], recv_sem.at[12])
+        arrived(ext.at[0], recv_sem.at[13])
+
+    for i in range(2):
+        project(partner_slot + i, None)
+
+    look([behind, behind + 1], [partner_slot - reach, partner_slot - reach + 1, -1, planes], True)
+    finish(0)
+    finish(2)
 
     for sem in range(8):
         arrived(others, send_sem.at[sem])
@@ -486,11 +557,13 @@
                 pltpu.VMEM((planes, blocks, 8, width), BF16),
                 pltpu.VMEM((deep, blocks, 8, width), BF16),
                 pltpu.VMEM((planes, tokens, width), BF16),
-                pltpu.VMEM((deep, tokens, width), BF16),
-                pltpu.VMEM((deep, tokens, width), BF16),
-                pltpu.VMEM((planes, tokens, width), BF16),
+                pltpu.VMEM((deep, 4, 64, width), BF16),
+                pltpu.VMEM((deep, 4, 64, width), BF16),
                 pltpu.VMEM((8, 128, 128), F32),
-                pltpu.VMEM((33, 128, 128), F32),
+                pltpu.VMEM((16, 25, 32, 128), F32),
+                pltpu.VMEM((2, 4, planes, 32, 128), F32),
+                pltpu.VMEM((2, 4, planes, 32, 128), F32),
+                pltpu.VMEM((2, 4, planes, 32, 128), F32),
                 pltpu.SemaphoreType.DMA((4,)),
                 pltpu.SemaphoreType.DMA((9,)),
                 pltpu.SemaphoreType.DMA((4,)),

time: 26 us -> 26.2 us (level)
  the two profiles are of different devices: /device:TPU:96 before, /device:TPU:1 now
where the time goes in v7:
time: 26.2 us; the launch traced here: 26.1 us
  Pallas kernels  25.3 us (97%)
  other arithmetic  0.73 us (3%)
    pallas_call x1, Pallas kernels, local(): pl.pallas_call(functools.partial(kernel, bins, slabs), out_shape=pltpu.VM...  25.3 us
    convert_element_type x1, other arithmetic, local(): return result.astype(BF16).reshape(volume.shape)  0.73 us

profile of v7, /device:TPU:1, one launch (start us, length us, event | category | flops | bytes accessed | tf_op | source)
XLA Modules:
  0.0 26.1 jit_solution(5287407009192680302)
XLA Ops:
  0.0 25.3 %shard_map.136 = f32[4,128,256]{2,1,0:T(8,128)S(1)} custom-call(s32[16]{0:T(128)} %bin_phase_hbm.1, f32[8,16]{1,0:T(8,128)} %phase_bias_hbm.1, s32[3,8]{1,0:T(4,128)} %bitcast.7, f32[8,64]{1,0:T(8,128)} %window_bias_hbm.1, f32[1,256]{1,0:T(1,128)} %bitcast.8, f32[1,256]{1,0:T(1,128)} %bitcast.9, f32[1,256]{1,0:T(1,128)} %bitcast.10, ...), custom_call_target="tpu_custom_call" | custom-call | tf_op jit(solution)/shard_map/pallas_call | solution.py:542
  25.3 0.7 %convert_element_type.3 = bf16[4,128,256]{2,1,0:T(8,128)(2,1)} convert(f32[4,128,256]{2,1,0:T(8,128)S(1)} %shard_map.136) | non-fusion elementwise | flops 131072 | bytes 786432 | tf_op jit(solution)/shard_map/convert_element_type | solution.py:586

commit v8 on v7

--- a/solution.py
+++ b/solution.py
@@ -90,12 +90,19 @@
     not_last = slab < slabs - 1
 
     barrier = pltpu.get_barrier_semaphore()
-
-    @pl.loop(1, bins)
-    def _(i):
-        pl.semaphore_signal(
-            barrier, inc=1, device_id={"phase": lax.rem(me + i, bins)}, device_id_type=MESH
-        )
+    assert bins == 16
+    flips = [v * (1 - 2 * lax.rem(lax.div(me, v), 2)) for v in (1, 2, 4, 8)]
+    peers = [
+        me + sum(flips[j] for j in range(4) if m >> j & 1)
+        for m in (12, 13, 4, 5, 10, 11, 14, 15, 8, 9, 2, 3, 6, 7, 1)
+    ]
+    slab_peers = [
+        me + sum(flips[j] for j in range(4) if m >> j & 1)
+        for m in (4, 5, 12, 13, 2, 3, 6, 7, 0, 1, 10, 11, 14, 15, 8, 9)
+    ]
+
+    for peer in peers:
+        pl.semaphore_signal(barrier, inc=1, device_id={"phase": peer}, device_id_type=MESH)
 
     @pl.when(not_first)
     def _():
@@ -175,9 +182,7 @@
     pl.semaphore_wait(barrier, bins - 1 + sides)
 
     def gather(plane):
-        @pl.loop(1, bins)
-        def _(i):
-            peer = lax.rem(me + i, bins)
+        for peer in peers:
             pltpu.make_async_remote_copy(
                 src_ref=vol.at[plane, peer],
                 dst_ref=got.at[plane, me],
@@ -264,8 +269,7 @@
             sent.at[plane, me], ext.at[reach + plane, me], own_sem.at[plane]
         ).start()
 
-        for i in range(1, bins):
-            peer = lax.rem(me + i, bins)
+        for peer in peers:
             pltpu.make_async_remote_copy(
                 src_ref=sent.at[plane, peer],
                 dst_ref=ext.at[reach + plane, me],
@@ -276,8 +280,7 @@
             ).start()
 
     def to_slab(plane, slot, target, sem):
-        for i in range(bins):
-            peer = lax.rem(me + i, bins)
+        for peer in slab_peers:
             pltpu.make_async_remote_copy(
                 src_ref=sent.at[plane, peer],
                 dst_ref=ext.at[slot, me],

time: 26.2 us -> 25.8 us (0.985)
  Pallas kernels: 25.3 us -> 24.9 us
    pallas_call x1, Pallas kernels: 25.3 us -> 24.9 us  [local(): pl.pallas_call(functools.partial(kernel, bins, slabs), out_shape=pltpu.VM...]
where the time goes in v8:
time: 25.8 us; the launch traced here: 25.7 us
  Pallas kernels  24.9 us (97%)
  other arithmetic  0.73 us (3%)
    pallas_call x1, Pallas kernels, local(): pl.pallas_call(functools.partial(kernel, bins, slabs), out_shape=pltpu.VM...  24.9 us
    convert_element_type x1, other arithmetic, local(): return result.astype(BF16).reshape(volume.shape)  0.73 us

profile of v8, /device:TPU:1, one launch (start us, length us, event | category | flops | bytes accessed | tf_op | source)
XLA Modules:
  0.0 25.7 jit_solution(9243591394053427890)
XLA Ops:
  0.0 24.9 %shard_map.136 = f32[4,128,256]{2,1,0:T(8,128)S(1)} custom-call(s32[16]{0:T(128)} %bin_phase_hbm.1, f32[8,16]{1,0:T(8,128)} %phase_bias_hbm.1, s32[3,8]{1,0:T(4,128)} %bitcast.7, f32[8,64]{1,0:T(8,128)} %window_bias_hbm.1, f32[1,256]{1,0:T(1,128)} %bitcast.8, f32[1,256]{1,0:T(1,128)} %bitcast.9, f32[1,256]{1,0:T(1,128)} %bitcast.10, ...), custom_call_target="tpu_custom_call" | custom-call | tf_op jit(solution)/shard_map/pallas_call | solution.py:545
  25.0 0.7 %convert_element_type.3 = bf16[4,128,256]{2,1,0:T(8,128)(2,1)} convert(f32[4,128,256]{2,1,0:T(8,128)S(1)} %shard_map.136) | non-fusion elementwise | flops 131072 | bytes 786432 | tf_op jit(solution)/shard_map/convert_element_type | solution.py:589

commit v9 on v8

--- a/solution.py
+++ b/solution.py
@@ -452,15 +452,21 @@
     def _():
         arrived(ext.at[0], recv_sem.at[10])
 
+    @pl.when(takes)
+    def _():
+        arrived(ext.at[0], recv_sem.at[12])
+        arrived(ext.at[0], recv_sem.at[13])
+
     for slot in (low + reach - 1, high):
         project(slot, None)
-
+    for i in range(2):
+        project(partner_slot + i, None)
+
+    for copy in weight_copies[5:]:
+        copy.wait()
     ahead = jnp.where(even, 2, 0)
     behind = 2 - ahead
     look([ahead, ahead + 1], [held_slot - reach, held_slot - reach + 1, -1, planes], True)
-    for copy in weight_copies[5:]:
-        copy.wait()
-
     def finish(first):
         rows = []
         for j in range(2):
@@ -483,14 +489,6 @@
         final = residual + dot(hidden.astype(BF16), w_down[...])
         out[pl.ds(first, 2)] = final.reshape(2, 128, 256)
 
-
-    @pl.when(takes)
-    def _():
-        arrived(ext.at[0], recv_sem.at[12])
-        arrived(ext.at[0], recv_sem.at[13])
-
-    for i in range(2):
-        project(partner_slot + i, None)
 
     look([behind, behind + 1], [partner_slot - reach, partner_slot - reach + 1, -1, planes], True)
     finish(0)

time: 25.8 us -> 25.4 us (0.984)
  Pallas kernels: 24.9 us -> 24.5 us
    pallas_call x1, Pallas kernels: 24.9 us -> 24.5 us  [local(): pl.pallas_call(functools.partial(kernel, bins, slabs), out_shape=pltpu.VM...]
where the time goes in v9:
time: 25.4 us; the launch traced here: 25.2 us
  Pallas kernels  24.5 us (96%)
  other arithmetic  0.73 us (3%)
    pallas_call x1, Pallas kernels, local(): pl.pallas_call(functools.partial(kernel, bins, slabs), out_shape=pltpu.VM...  24.5 us
    convert_element_type x1, other arithmetic, local(): return result.astype(BF16).reshape(volume.shape)  0.73 us

profile of v9, /device:TPU:1, one launch (start us, length us, event | category | flops | bytes accessed | tf_op | source)
XLA Modules:
  0.0 25.2 jit_solution(6764081599463563286)
XLA Ops:
  0.0 24.5 %shard_map.136 = f32[4,128,256]{2,1,0:T(8,128)S(1)} custom-call(s32[16]{0:T(128)} %bin_phase_hbm.1, f32[8,16]{1,0:T(8,128)} %phase_bias_hbm.1, s32[3,8]{1,0:T(4,128)} %bitcast.7, f32[8,64]{1,0:T(8,128)} %window_bias_hbm.1, f32[1,256]{1,0:T(1,128)} %bitcast.8, f32[1,256]{1,0:T(1,128)} %bitcast.9, f32[1,256]{1,0:T(1,128)} %bitcast.10, ...), custom_call_target="tpu_custom_call" | custom-call | tf_op jit(solution)/shard_map/pallas_call | solution.py:543
  24.5 0.7 %convert_element_type.3 = bf16[4,128,256]{2,1,0:T(8,128)(2,1)} convert(f32[4,128,256]{2,1,0:T(8,128)S(1)} %shard_map.136) | non-fusion elementwise | flops 131072 | bytes 786432 | tf_op jit(solution)/shard_map/convert_element_type | solution.py:587

commit v10 on v9

--- a/solution.py
+++ b/solution.py
@@ -487,7 +487,7 @@
         level = 0.5 * rise
         hidden = level + level * bend
         final = residual + dot(hidden.astype(BF16), w_down[...])
-        out[pl.ds(first, 2)] = final.reshape(2, 128, 256)
+        out[pl.ds(first, 2)] = final.astype(BF16).reshape(2, 128, 256)
 
 
     look([behind, behind + 1], [partner_slot - reach, partner_slot - reach + 1, -1, planes], True)
@@ -542,7 +542,7 @@
         weights = (phase_qkv, phase_out, window_qkv, window_out, mlp_up, mlp_down)
         result = pl.pallas_call(
             functools.partial(kernel, bins, slabs),
-            out_shape=pltpu.VMEM((planes, tokens, width), F32),
+            out_shape=pltpu.VMEM((planes, tokens, width), BF16),
             in_specs=[hbm] * 14,
             out_specs=vmem,
             scratch_shapes=[
@@ -584,7 +584,7 @@
             volume.reshape(planes, blocks, 8, width),
             *weights,
         )
-        return result.astype(BF16).reshape(volume.shape)
+        return result.reshape(volume.shape)
 
     split = P("phase", "space", None, None, None)
     return jax.shard_map(

time: 25.4 us -> 25.4 us (level)
  other arithmetic: 0.73 us -> 0 us
  local copies, waits for them, and re-layouts: 0 us -> 0.71 us
    convert_element_type x1 -> x0, other arithmetic: 0.73 us -> none  [local(): return result.astype(BF16).reshape(volume.shape)]
    unnamed x0 -> x1, local copies, waits for them, and re-layouts: none -> 0.71 us
where the time goes in v10:
time: 25.4 us; the launch traced here: 25.2 us
  Pallas kernels  24.5 us (96%)
  local copies, waits for them, and re-layouts  0.71 us (3%)
    pallas_call x1, Pallas kernels, local(): pl.pallas_call(functools.partial(kernel, bins, slabs), out_shape=pltpu.VM...  24.5 us
    unnamed x1, local copies, waits for them, and re-layouts  0.71 us

profile of v10, /device:TPU:1, one launch (start us, length us, event | category | flops | bytes accessed | tf_op | source)
XLA Modules:
  0.0 25.2 jit_solution(822615702640800748)
XLA Ops:
  0.0 24.5 %shard_map.136 = bf16[4,128,256]{2,1,0:T(8,128)(2,1)S(1)} custom-call(s32[16]{0:T(128)} %bin_phase_hbm.1, f32[8,16]{1,0:T(8,128)} %phase_bias_hbm.1, s32[3,8]{1,0:T(4,128)} %bitcast.8, f32[8,64]{1,0:T(8,128)} %window_bias_hbm.1, f32[1,256]{1,0:T(1,128)} %bitcast.9, f32[1,256]{1,0:T(1,128)} %bitcast.10, f32[1,256]{1,0:T(1,128)} %bitcast.11, ...), custom_call_target="tpu_custom_call" | custom-call | tf_op jit(solution)/shard_map/pallas_call | solution.py:543
  24.5 0.7 %copy.16 = bf16[1,4,4,32,256]{4,3,2,1,0:T(8,128)(2,1)} copy(bf16[1,4,4,32,256]{4,3,2,1,0:T(8,128)(2,1)S(1)} %bitcast.6) | data formatting | bytes 524288
